TPU v7x, 32 devices: a whole 2x2x4 slice. The times are simulated.
32 devices in a mesh: cores: 2 (over core), row: 4 (over y, x), vec: 4 (over z).
Axes of the slice: x: 2, y: 2, z: 4, core: 2. Of those that a mesh axis runs over, the one named last changes fastest.
Arguments:
- train_cores: float32 [4, 512, 256, 256], P('vec', 'cores', 'row'), may hold values from -0.01953125 to 0.01953125
- sketch: float32 [512, 128], P('cores'), may hold values from -6 to 6
- exit_sketch: float32 [256, 128], replicated, may hold values from -6 to 6
Outputs:
- rounded: float32 [4, 256, 256, 128], P('vec', 'cores', 'row')
- interface_bases: float32 [4, 512, 128], P('vec', 'cores')
- margins: float32 [4, 256, 512], P('vec', 'cores')
All inputs are finite; a program needn't handle non-finite values.
Results may differ from a plain program's by a relative error of at most 0.0003.
Values sent between devices are 32-bit elements; how exact they have to be, the bound alone decides.
No kernel may reach another device: no remote copies, remote signals or barrier semaphores. Data moves between devices by JAX's collectives and lax.ppermute only.
A program may use at most 192 MiB of HBM per device.

v0:
```python
import functools
import math

import jax
import jax.numpy as jnp
from jax import lax
from jax.experimental import pallas as pl
from jax.experimental.pallas import tpu as pltpu
from jax.sharding import PartitionSpec as P


MODE = 256
F32 = jnp.float32
BF16 = jnp.bfloat16
BASIS_UNROLL = 2


def contract(left, right, left_dim, right_dim, precision=None):
    return lax.dot_general(
        left,
        right,
        (((left_dim,), (right_dim,)), ((), ())),
        precision=precision,
        preferred_element_type=F32,
    )


exact = functools.partial(contract, precision=lax.Precision.HIGHEST)


def split(value):
    high = value.astype(BF16)
    return high, (value - high.astype(F32)).astype(BF16)


def tree_sum(terms):
    terms = list(terms)
    while len(terms) > 1:
        terms = [terms[i] + terms[i + 1] for i in range(0, len(terms), 2)]
    return terms[0]


def shape(dims, dtype=F32):
    return jax.ShapeDtypeStruct(dims, dtype)


def fixed(*dims):
    return pl.BlockSpec(dims, lambda *_: (0,) * len(dims))


def inverse_factor(gram, out_ref, unroll=1):
    size = gram.shape[0]
    row_id = lax.broadcasted_iota(jnp.int32, (size, size), 0)
    col_id = lax.broadcasted_iota(jnp.int32, (size, size), 1)
    inverse = jnp.where(row_id == col_id, 1.0, 0.0).astype(F32)
    done = 0
    while done < size:
        left = size - done
        panels = left // 16 if left > 16 * unroll else left // 8
        rows = row_id[:left]

        def panel(k, carry, left=left, done=done, rows=rows):
            gram, inverse = carry
            open_rows = rows < left - 8 * k
            columns = [jnp.broadcast_to(gram[:, t : t + 1], (left, size)) for t in range(8)]
            scale = jnp.zeros((8, size), F32)
            for t in range(8):
                pivot = columns[t][t : t + 1, :]
                factor = jnp.where((rows > t) & open_rows, columns[t] * (1.0 / pivot), 0.0)
                for s in range(t + 1, 8):
                    columns[s] = columns[s] - factor * columns[s][t : t + 1, :]
                gram = gram - factor * gram[t : t + 1, :]
                inverse = inverse - factor * inverse[t : t + 1, :]
                scale = jnp.where(rows[:8] == t, lax.rsqrt(pivot), scale)
            out_ref[pl.ds(pl.multiple_of(done + 8 * k, 8), 8), :] = inverse[:8] * scale
            gram = pltpu.roll(jnp.concatenate([gram[8:], gram[:8]], axis=0), size - 8, 1)
            return gram, jnp.concatenate([inverse[8:], inverse[:8]], axis=0)

        carry = (gram[:left], inverse[:left])
        gram, inverse = lax.fori_loop(0, panels, panel, carry, unroll=min(unroll, panels))
        done += 8 * panels
        gram, inverse = gram[: size - done], inverse[: size - done]


def write_halves(state_ref, value, keep_ref, give_ref):
    half = value.shape[0] // 2
    cut = half // 2
    first = jnp.concatenate([value[:half, :half], value[half : half + cut, :half]], axis=0)
    second = jnp.concatenate([value[half + cut :, :half], value[half:, half:]], axis=0)
    mine = state_ref[2] == 0
    keep_ref[...] = jnp.where(mine, first, second)
    give_ref[...] = jnp.where(mine, second, first)


def read_halves(state_ref, own_ref, other_ref):
    own, other = own_ref[...], other_ref[...]
    mine = state_ref[2] == 0
    first = jnp.where(mine, own, other)
    second = jnp.where(mine, other, own)
    half = own.shape[1]
    cut = half // 2
    cross = jnp.concatenate([first[half:], second[:cut]], axis=0)
    return first[:half], cross, second[cut:]


def whole(blocks):
    first, cross, second = blocks
    return jnp.concatenate(
        [jnp.concatenate([first, cross.T], axis=1), jnp.concatenate([cross, second], axis=1)],
        axis=0,
    )


def half_dims(rank):
    return (3 * rank // 4, rank // 2)


def gram_body(state_ref, core_ref, keep_ref, give_ref, acc_ref):
    step = pl.program_id(0)

    @pl.when(state_ref[0] == 1)
    def _():
        @pl.when(step == 0)
        def _():
            acc_ref[...] = jnp.zeros_like(acc_ref)

        rank, modes, width = core_ref.shape
        high, low = split(core_ref[...].reshape(rank * modes, width))
        acc_ref[...] += contract(high, jnp.concatenate([high, low], axis=1), 0, 0)

        @pl.when(step == pl.num_programs(0) - 1)
        def _():
            cross = acc_ref[:, width:]
            total = acc_ref[:, :width] + (cross + cross.T)
            write_halves(state_ref, total, keep_ref, give_ref)


def core_spec(rank, modes, width):
    return pl.BlockSpec((rank, modes, width), lambda s, state: (0, s * state[0], 0))


def gram(state, core):
    rank, mode_count, width = core.shape
    modes = min(16, mode_count)
    return pl.pallas_call(
        gram_body,
        grid_spec=pltpu.PrefetchScalarGridSpec(
            num_scalar_prefetch=1,
            grid=(mode_count // modes,),
            in_specs=[core_spec(rank, modes, width)],
            out_specs=[fixed(*half_dims(width))] * 2,
            scratch_shapes=[pltpu.VMEM((width, 2 * width), F32)],
        ),
        out_shape=[shape(half_dims(width))] * 2,
        name="gram",
    )(state, core)


def write_factor(state_ref, own_ref, other_ref, low_ref, inv_ref, work_ref):
    half = low_ref.shape[0] // 2
    first, cross, second = read_halves(state_ref, own_ref, other_ref)
    inverse_factor(first, work_ref)
    inv_first = work_ref[...]
    low_cross = exact(cross, inv_first, 1, 1)
    second = second - exact(low_cross, low_cross, 1, 1)
    inverse_factor(second, work_ref)
    inv_second = work_ref[...]
    zero = jnp.zeros((half, half), F32)
    low_ref[:half, :half] = exact(first, inv_first, 1, 1)
    low_ref[:half, half:] = zero
    low_ref[half:, :half] = low_cross
    low_ref[half:, half:] = exact(second, inv_second, 1, 1)
    inv_ref[:half, :half] = inv_first
    inv_ref[:half, half:] = zero
    inv_ref[half:, :half] = -exact(inv_second, exact(low_cross, inv_first, 1, 0), 1, 0)
    inv_ref[half:, half:] = inv_second


def absorbed_body(
    state_ref,
    own_ref,
    other_ref,
    core_ref,
    keep_ref,
    give_ref,
    low_ref,
    inv_ref,
    both_ref,
    acc_ref,
    mid_ref,
    work_ref,
):
    step = pl.program_id(0)

    @pl.when((state_ref[0] == 0) & (step == 0))
    def _():
        write_factor(state_ref, own_ref, other_ref, low_ref, inv_ref, work_ref)

    @pl.when(state_ref[0] == 1)
    def _():
        rank, modes, width = core_ref.shape

        @pl.when(step == 0)
        def _():
            acc_ref[...] = jnp.zeros_like(acc_ref)
            outer_high, outer_low = split(whole(read_halves(state_ref, own_ref, other_ref)))
            both_ref[:rank] = outer_high
            both_ref[rank:] = outer_low

        high, low = split(core_ref[...].transpose(1, 0, 2))
        both = both_ref[...]
        for i in range(modes):
            stacked = contract(both, high[i], 1, 0)
            rest = contract(both[:rank], low[i], 1, 0)
            main = stacked[:rank] + stacked[rank:]
            main_high = main.astype(BF16)
            mid_ref[i * rank : (i + 1) * rank, :width] = main_high
            mid_ref[i * rank : (i + 1) * rank, width:] = (
                (main - main_high.astype(F32)) * 0.5 + rest
            ).astype(BF16)
        acc_ref[...] += contract(high.reshape(modes * rank, width), mid_ref[...], 0, 0)

        @pl.when(step == pl.num_programs(0) - 1)
        def _():
            half = acc_ref[:, :width] * 0.5 + acc_ref[:, width:]
            write_halves(state_ref, half + half.T, keep_ref, give_ref)


def absorbed_gram(state, outer, core):
    rank, mode_count, width = core.shape
    modes = min(8, mode_count)
    return pl.pallas_call(
        absorbed_body,
        grid_spec=pltpu.PrefetchScalarGridSpec(
            num_scalar_prefetch=1,
            grid=(mode_count // modes,),
            in_specs=[fixed(*half_dims(rank))] * 2 + [core_spec(rank, modes, width)],
            out_specs=[fixed(*half_dims(width))] * 2 + [fixed(rank, rank)] * 2,
            scratch_shapes=[
                pltpu.VMEM((2 * rank, rank), BF16),
                pltpu.VMEM((width, 2 * width), F32),
                pltpu.VMEM((modes * rank, 2 * width), BF16),
                pltpu.VMEM((rank // 2, rank // 2), F32),
            ],
        ),
        out_shape=[shape(half_dims(width))] * 2 + [shape((rank, rank))] * 2,
        name="absorbed_gram",
    )(state, *outer, core)


def project_step(state_ref, core_ref, map_ref, high_ref, low_ref, keep_ref, give_ref, both_ref, acc_ref):
    step = pl.program_id(0)
    rank, modes, width = core_ref.shape
    kept = map_ref.shape[1]

    @pl.when(step == 0)
    def _():
        acc_ref[...] = jnp.zeros_like(acc_ref)
        map_high, map_low = split(map_ref[...])
        both_ref[:, :kept] = map_high
        both_ref[:, kept:] = map_low

    high, low = split(core_ref[...].reshape(rank * modes, width))
    both = both_ref[...]
    first = contract(high, both, 1, 0)
    second = contract(low, both, 1, 0)
    mixed = first[:, :kept] + (first[:, kept:] + second[:, :kept])
    mixed = mixed.reshape(rank, modes, kept).transpose(1, 0, 2)
    mixed = jnp.concatenate([mixed[i] for i in range(modes)], axis=1)
    mixed_high, mixed_low = split(mixed)
    high_ref[...] = mixed_high
    low_ref[...] = mixed_low
    acc_ref[...] += contract(mixed_high, jnp.concatenate([mixed_high, mixed_low], axis=0), 1, 1)

    @pl.when(step == pl.num_programs(0) - 1)
    def _():
        cross = acc_ref[:, rank:]
        total = acc_ref[:, :rank] + (cross + cross.T)
        write_halves(state_ref, total, keep_ref, give_ref)


def shaped_piece(front_ref, high_ref, low_ref):
    kept = front_ref.shape[1]
    front_high, front_low = split(front_ref[...].T)
    both = jnp.concatenate([front_high, front_low], axis=0)
    first = contract(both, high_ref[...], 1, 0)
    second = contract(front_high, low_ref[...], 1, 0)
    return first[:kept] + (first[kept:] + second)


def project_body(pieces, state_ref, *refs):
    core_ref, map_ref, refs = refs[0], refs[1], refs[2:]
    if pieces:
        other_refs, refs = refs[:3], refs[3:]
        piece_refs, slots_ref, copied = refs[4 : 4 + pieces], refs[-2], refs[-1]
    high_ref, low_ref, keep_ref, give_ref = refs[:4]
    both_ref, acc_ref = refs[4 + pieces : 6 + pieces]

    @pl.when(state_ref[0] == 1)
    def _():
        project_step(
            state_ref, core_ref, map_ref, high_ref, low_ref, keep_ref, give_ref, both_ref, acc_ref
        )

    if pieces:

        @pl.when(state_ref[0] == 0)
        def _():
            step = pl.program_id(0)
            slots_ref[step] = shaped_piece(*other_refs)
            copies = [
                pltpu.make_async_copy(slots_ref.at[d], piece_refs[d], copied.at[d])
                for d in range(pieces)
            ]
            for d in range(pieces):

                @pl.when(step == d)
                def _(d=d):
                    copies[d].start()

            @pl.when(step == pieces - 1)
            def _():
                for copy in copies:
                    copy.wait()


def project(state, core, right_map, other=None, pieces=0):
    rank, mode_count, width = core.shape
    kept = right_map.shape[1]
    modes = mode_count // pieces if pieces else min(16, mode_count)
    wide = pl.BlockSpec((rank, modes * kept), lambda s, state: (0, s * state[0]))
    in_specs = [core_spec(rank, modes, width), fixed(width, kept)]
    out_specs = [wide, wide] + [fixed(*half_dims(rank))] * 2
    out_shape = [shape((rank, mode_count * kept), BF16)] * 2 + [shape(half_dims(rank))] * 2
    scratch = [pltpu.VMEM((width, 2 * kept), BF16), pltpu.VMEM((rank, 2 * rank), F32)]
    operands = [core, right_map]
    if pieces:
        away = pl.BlockSpec(
            (rank, modes * kept), lambda s, state: (0, state[1] ^ (s * (1 - state[0])))
        )
        in_specs += [fixed(rank, kept), away, away]
        operands += other
        out_specs += [pl.BlockSpec(memory_space=pl.ANY)] * pieces
        out_shape += [shape((kept, modes * kept))] * pieces
        scratch += [
            pltpu.VMEM((pieces, kept, modes * kept), F32),
            pltpu.SemaphoreType.DMA((pieces,)),
        ]
    return pl.pallas_call(
        functools.partial(project_body, pieces),
        grid_spec=pltpu.PrefetchScalarGridSpec(
            num_scalar_prefetch=1,
            grid=(mode_count // modes,),
            in_specs=in_specs,
            out_specs=out_specs,
            scratch_shapes=scratch,
        ),
        out_shape=out_shape,
        name="project",
    )(state, *operands)


SMEM = pl.BlockSpec(memory_space=pltpu.SMEM)
VMEM = pl.BlockSpec(memory_space=pltpu.VMEM)


def basis_body(absorbed, state_ref, own_ref, other_ref, *refs):
    if absorbed:
        sketch_ref, low_ref, inv_ref, basis_ref, front_ref, map_ref, work_ref = refs
    else:
        sketch_ref, basis_ref, work_ref = refs

    @pl.when(state_ref[0] == 1)
    def _():
        total = whole(read_halves(state_ref, own_ref, other_ref))
        if absorbed:
            lower = low_ref[...]
            total = exact(exact(lower, total, 0, 0), lower, 1, 0)
        powered = exact(total, exact(total, sketch_ref[...], 1, 0), 1, 0)
        inverse_factor(exact(powered, powered, 0, 0), work_ref, BASIS_UNROLL)
        frame = exact(powered, work_ref[...], 1, 1)
        basis_ref[...] = frame
        if absorbed:
            front_ref[...] = exact(lower, frame, 1, 0)
            map_ref[...] = exact(inv_ref[...], frame, 0, 0)


def basis(state, halves, sketch, lower=None, inverse=None):
    absorbed = lower is not None
    operands = (*halves, sketch) + ((lower, inverse) if absorbed else ())
    kept = sketch.shape[1]
    return pl.pallas_call(
        functools.partial(basis_body, absorbed),
        in_specs=[SMEM] + [VMEM] * len(operands),
        out_shape=[shape(sketch.shape)] * (3 if absorbed else 1),
        scratch_shapes=[pltpu.VMEM((kept, kept), F32)],
        name="basis",
    )(state, *operands)


def piece_body(state_ref, front_ref, high_ref, low_ref, piece_ref):
    @pl.when(state_ref[0] == 1)
    def _():
        piece_ref[...] = shaped_piece(front_ref, high_ref, low_ref)


def round_piece(state, front, high, low, pieces):
    rank, wide = high.shape
    kept = front.shape[1]
    width = wide // pieces
    parts = 2 if width % 2048 == 0 else 1
    block = pl.BlockSpec(
        (rank, width // parts), lambda s, state: (0, (state[1] * parts + s) * state[0])
    )
    return pl.pallas_call(
        piece_body,
        grid_spec=pltpu.PrefetchScalarGridSpec(
            num_scalar_prefetch=1,
            grid=(parts,),
            in_specs=[fixed(rank, kept), block, block],
            out_specs=pl.BlockSpec((kept, width // parts), lambda s, state: (0, s * state[0])),
        ),
        out_shape=shape((kept, width)),
        name="round_piece",
    )(state, front, high, low)


def layout_body(pieces, scale, state_ref, *refs):
    sides, (out_ref, slots_ref, laid_ref, taken, placed) = (
        (refs[:pieces], refs[pieces : 2 * pieces]),
        refs[2 * pieces :],
    )
    vec = state_ref[1]
    for side in (0, 1):

        @pl.when(state_ref[2] == side)
        def _(side=side):
            copies = [
                pltpu.make_async_copy(sides[side][d], slots_ref.at[d], taken.at[d])
                for d in range(pieces)
            ]
            for copy in copies:
                copy.start()
            for copy in copies:
                copy.wait()

    kept, modes = laid_ref.shape[1:3]
    copies = []
    for d in range(pieces):
        stacked = jnp.stack(
            [slots_ref[d, :, i * kept : (i + 1) * kept] for i in range(modes)], axis=0
        )
        laid_ref[d] = stacked.transpose(1, 0, 2) * scale
        copies.append(pltpu.make_async_copy(laid_ref.at[d], out_ref.at[:, vec ^ d], placed.at[d]))
        copies[-1].start()
    for copy in copies:
        copy.wait()


def lay_out(state, first, last, scale):
    pieces = len(first)
    kept, width = first[0].shape
    modes = width // kept
    anywhere = pl.BlockSpec(memory_space=pl.ANY)
    return pl.pallas_call(
        functools.partial(layout_body, pieces, scale),
        in_specs=[SMEM] + [anywhere] * (2 * pieces),
        out_specs=anywhere,
        out_shape=shape((kept, pieces, modes, kept)),
        scratch_shapes=[
            pltpu.VMEM((pieces, kept, width), F32),
            pltpu.VMEM((pieces, kept, modes, kept), F32),
            pltpu.SemaphoreType.DMA((pieces,)),
            pltpu.SemaphoreType.DMA((pieces,)),
        ],
        name="lay_out",
    )(state, *first, *last)


def pair_list(count):
    return [(p, q) for p in range(count) for q in range(p, count)]


def place_chunks(state_ref, own_ref, other_ref, out_ref):
    chunks, size = own_ref.shape[:2]
    side, row = state_ref[2], state_ref[3]
    for d in range(chunks):
        for ref, half in ((own_ref, side), (other_ref, 1 - side)):
            start = pl.multiple_of((half * chunks + (row ^ d)) * size, 8)
            out_ref[pl.ds(start, size), :] = ref[d]


def margin_body(count, first, state_ref, *refs):
    piece_refs, refs = refs[:count], refs[count:]
    if first:
        frame_refs, refs = refs[:count], refs[count:]
        keep_ref, give_ref, stage_ref, env_ref, out_ref, frame_stage_ref = refs
    else:
        own_ref, other_ref, keep_ref, give_ref, stage_ref, env_ref, out_ref, env_in_ref = refs
    step = pl.program_id(0)
    pairs = pair_list(count)
    index_of = {pair: i for i, pair in enumerate(pairs)}

    @pl.when(state_ref[0] == 1)
    def _():
        me = state_ref[1]
        kept = piece_refs[0].shape[0]

        @pl.when(step == 0)
        def _():
            out_ref[...] = jnp.zeros_like(out_ref)
            if first:
                for d in range(count):
                    frame_stage_ref[me ^ d] = frame_refs[d][...]
            else:
                place_chunks(state_ref, own_ref, other_ref, env_in_ref)
            for i, (p, q) in enumerate(pairs):
                if first:
                    env = exact(frame_stage_ref[p], frame_stage_ref[q], 0, 0)
                else:
                    env = env_in_ref[i * kept : (i + 1) * kept]
                env_high, env_low = split(env)
                env_ref[q, p * kept : (p + 1) * kept] = env_high
                env_ref[q, (count + p) * kept : (count + p + 1) * kept] = env_low

        for d in range(count):
            stage_ref[me ^ d] = piece_refs[d][...]
        modes = piece_refs[0].shape[1] // kept

        def tall(value):
            return jnp.concatenate(
                [value[:, i * kept : (i + 1) * kept] for i in range(modes)], axis=0
            )

        highs, lows, carried = [], [], {}
        for q in range(count):
            high, low = split(stage_ref[q])
            highs.append(tall(high))
            lows.append(tall(low))
            rows = (q + 1) * kept
            env_high = env_ref[q, :rows]
            env_low = env_ref[q, count * kept : count * kept + rows]
            stacked = contract(jnp.concatenate([env_high, env_low], axis=0), high, 1, 0)
            moved = stacked[:rows] + (stacked[rows:] + contract(env_high, low, 1, 0))
            for p in range(q + 1):
                carried[p, q] = split(tall(moved[p * kept : (p + 1) * kept]))
        for p in range(count):
            partners = range(p, count)
            main = contract(
                jnp.concatenate([highs[p], lows[p]], axis=1),
                jnp.concatenate([carried[p, q][0] for q in partners], axis=1),
                0,
                0,
            )
            cross = contract(
                highs[p], jnp.concatenate([carried[p, q][1] for q in partners], axis=1), 0, 0
            )
            total = main[:kept] + (main[kept:] + cross)
            for j, q in enumerate(partners):
                i = index_of[p, q]
                out_ref[i * kept : (i + 1) * kept] += total[:, j * kept : (j + 1) * kept]

        @pl.when(step == pl.num_programs(0) - 1)
        def _():
            chunks, size = keep_ref.shape[:2]
            side, row = state_ref[2], state_ref[3]
            for d in range(chunks):
                for ref, half in ((keep_ref, side), (give_ref, 1 - side)):
                    start = pl.multiple_of((half * chunks + (row ^ d)) * size, 8)
                    ref[d] = out_ref[pl.ds(start, size), :]


def margin_terms(state, pieces, rows, frames=None, env=None):
    count = len(pieces)
    kept, wide = pieces[0].shape
    chunk = min(4 * kept, wide)
    first = frames is not None
    total = count * (count + 1) // 2 * kept
    piece_spec = pl.BlockSpec((kept, chunk), lambda s, state: (0, s * state[0]))
    extra = list(frames) if first else list(env)
    part = (rows, total // (2 * rows), kept)
    scratch = [
        pltpu.VMEM((count, kept, chunk), F32),
        pltpu.VMEM((count, 2 * count * kept, kept), BF16),
        pltpu.VMEM((total, kept), F32),
        pltpu.VMEM((count, *frames[0].shape) if first else (total, kept), F32),
    ]
    return pl.pallas_call(
        functools.partial(margin_body, count, first),
        grid_spec=pltpu.PrefetchScalarGridSpec(
            num_scalar_prefetch=1,
            grid=(wide // chunk,),
            in_specs=[piece_spec] * count + [fixed(*x.shape) for x in extra],
            out_specs=[fixed(*part)] * 2,
            scratch_shapes=scratch,
        ),
        out_shape=[shape(part)] * 2,
        name="margin_terms",
    )(state, *pieces, *extra)


def pick_body(count, state_ref, *refs):
    out_ref, env_ref = refs[4:]
    kept = out_ref.shape[0]
    me = state_ref[1]
    for side in (0, 1):

        @pl.when(state_ref[2] == side)
        def _(side=side):
            place_chunks(state_ref, refs[2 * side], refs[2 * side + 1], env_ref)

    for q in range(count):
        low, high = jnp.minimum(me, q), jnp.maximum(me, q)
        index = low * count - low * (low - 1) // 2 + high - low
        block = env_ref[pl.ds(pl.multiple_of(index * kept, kept), kept), :]
        block = jnp.where(me > q, block.T, block)
        out_ref[:, q * kept : (q + 1) * kept] = block


def pick(state, env_first, env_last, count):
    kept = env_first[0].shape[2]
    return pl.pallas_call(
        functools.partial(pick_body, count),
        in_specs=[SMEM] + [VMEM] * 4,
        out_shape=shape((kept, count * kept)),
        scratch_shapes=[pltpu.VMEM((count * (count + 1) // 2 * kept, kept), F32)],
        name="pick",
    )(state, *env_first, *env_last)


def send(block, axis, size, distance):
    return lax.ppermute(block, axis, [(i, i ^ distance) for i in range(size)])


def swap(block):
    return send(block, "cores", 2, 1)


def send_from(block, side, size, distance):
    pairs = [(side * size + i, side * size + (i ^ distance)) for i in range(size)]
    return lax.ppermute(block, ("cores", "vec"), pairs)


def exchange_sum(block, axis, size):
    return tree_sum([block] + [send(block, axis, size, d) for d in range(1, size)])


def local(train_cores, sketch, exit_sketch):
    core = train_cores[0]
    rank, mode_count, _ = core.shape
    kept = sketch.shape[1]
    row_size = lax.axis_size("row")
    vec_size = lax.axis_size("vec")
    side = lax.axis_index("cores")
    row = lax.axis_index("row")
    vec = lax.axis_index("vec")
    first_side = (side == 0).astype(jnp.int32)
    state_first = jnp.stack([first_side, vec, side, row])
    state_last = jnp.stack([1 - first_side, vec, side, row])
    state_both = jnp.stack([jnp.int32(1), vec, side, row])
    scale = math.sqrt(kept * MODE)

    def row_total(keep, give, holder):
        mine = jnp.where(side == holder, keep, swap(give))
        own = exchange_sum(mine, "row", row_size)
        return own, swap(own)

    def env_total(keep, give, holder):
        mine = jnp.where(side == holder, keep, swap(give))
        parts = [mine[0]] + [send(mine[d], "row", row_size, d) for d in range(1, row_size)]
        chunk = exchange_sum(tree_sum(parts), "vec", vec_size)
        own = jnp.stack([chunk] + [send(chunk, "row", row_size, d) for d in range(1, row_size)])
        return own, swap(own)

    def at(state, d):
        return state.at[1].set(vec ^ d)

    def sent(pieces, holder):
        out = [pieces[0]]
        for d in range(1, vec_size):
            out.append(send_from(pieces[d], holder, vec_size, d))
        return out

    gram_first = row_total(*gram(state_first, core), 0)
    *gram_last, lower, inverse = absorbed_gram(state_last, gram_first, core)
    gram_last = row_total(*gram_last, 1)
    lower = jnp.where(side == 0, lower, swap(lower))
    inverse = jnp.where(side == 0, inverse, swap(inverse))
    (exit_frame,) = basis(state_last, gram_last, exit_sketch)
    last_high, last_low, *left_last = project(state_last, core, exit_frame)
    left_last = row_total(*left_last, 1)
    other_sketch = swap(sketch)
    frame_last, front, map_first = basis(
        state_both, left_last, jnp.where(side == 1, sketch, other_sketch), lower, inverse
    )
    rounded_last = [front, last_high, last_low]
    if mode_count // vec_size % 8 == 0:
        first_high, first_low, *rest = project(
            state_first, core, map_first, rounded_last, vec_size
        )
        left_first, own_last = rest[:2], rest[2:]
    else:
        first_high, first_low, *left_first = project(state_first, core, map_first)
        own_last = [
            round_piece(at(state_last, d), *rounded_last, vec_size) for d in range(vec_size)
        ]
    left_first = row_total(*left_first, 0)
    *own_last, left_own, left_other = lax.optimization_barrier((*own_last, *left_first))
    pieces_last = sent(own_last, 1)
    (frame_first,) = basis(state_first, (left_own, left_other), sketch)
    own_first = [None] * vec_size
    for d in range(vec_size - 1, -1, -1):
        own_first[d] = round_piece(at(state_first, d), frame_first, first_high, first_low, vec_size)
    pieces_first = sent(own_first, 0)
    rounded = lay_out(state_both, own_first, own_last, scale)
    frames = [frame_first] + [send_from(frame_first, 0, vec_size, d) for d in range(1, vec_size)]
    env_first = env_total(*margin_terms(state_first, pieces_first, row_size, frames=frames), 0)
    env_last = env_total(*margin_terms(state_last, pieces_last, row_size, env=env_first), 1)
    margins = pick(state_both, env_first, env_last, vec_size)
    bases = jnp.where(side == 0, frame_first, frame_last) * math.sqrt(rank)
    return rounded.reshape(1, kept, mode_count, kept), bases[None], margins[None]


def solution(mesh):
    return jax.shard_map(
        local,
        mesh=mesh,
        in_specs=(P("vec", "cores", "row", None), P("cores", None), P()),
        out_specs=(
            P("vec", "cores", "row", None),
            P("vec", "cores", None),
            P("vec", "cores", None),
        ),
        check_vma=False,
    )
```

profile of v0, /device:TPU:0, one launch (start us, length us, event | category | flops | bytes accessed | tf_op | source)
XLA Modules:
  0.0 336.5 jit_solution(15661034154628115718)
XLA Ops:
  1.3 10.1 %gram.1 = (f32[192,128]{1,0:T(8,128)}, f32[192,128]{1,0:T(8,128)}) custom-call(s32[4]{0:T(128)} %add_add_fusion.7.state_ref, f32[256,64,256]{2,1,0:T(8,128)} %bitcast.45), custom_call_target="tpu_custom_call" | custom-call | tf_op jit(solution)/shard_map/gram/pallas_call | solution.py:145
  13.7 3.0 collective-permute-start.1
  19.5 2.9 collective-permute-done.2
  25.9 16.8 %absorbed_gram.1 = (f32[192,128]{1,0:T(8,128)}, f32[192,128]{1,0:T(8,128)}, f32[256,256]{1,0:T(8,128)}, f32[256,256]{1,0:T(8,128)}) custom-call(s32[4]{0:T(128)} %add_add_fusion.8.state_ref, f32[192,128]{1,0:T(8,128)} %copy-done.12, f32[192,128]{1,0:T(8,128)} %copy-done.22, f32[256,64,256]{2,1,0:T(8,128)} %bitcast.46), custom_call_target="tpu_custom_call" | custom-call | tf_op jit(solution)/shard_map/absorbed_gram/pallas_call | solution.py:232
  46.0 2.5 collective-permute-start.8
  50.3 2.9 collective-permute-done.7
  55.3 1.9 basis.3.refs_1_
  57.2 4.5 %project.2 = (bf16[256,8192]{1,0:T(8,128)(2,1)}, bf16[256,8192]{1,0:T(8,128)(2,1)}, f32[192,128]{1,0:T(8,128)}, f32[192,128]{1,0:T(8,128)}) custom-call(s32[4]{0:T(128)} %add_add_fusion.8.state_ref, f32[256,64,256]{2,1,0:T(8,128)} %bitcast.47, f32[256,128]{1,0:T(8,128)} %basis.3.refs_1_), custom_call_target="tpu_custom_call" | custom-call | tf_op jit(solution)/shard_map/project/pallas_call | solution.py:349
  61.6 17.7 %collective-permute-start.10 = (f32[192,128]{1,0:T(8,128)}, f32[192,128]{1,0:T(8,128)S(1)}, u32[]{:S(2)}, u32[]{:S(2)}) collective-permute-start(f32[192,128]{1,0:T(8,128)} %get-tuple-element.87), channel_id=1, source_target_pairs={{0,16},{16,0},{1,17},{17,1},{2,18},{18,2},{3,19},{19,3},{4,20},{20... | collective-permute-start | bytes 294920 | tf_op jit(solution)/shard_map/ppermute | solution.py:632
  80.5 1.5 collective-permute-start.11
  86.0 3.9 %collective-permute-done.12 = f32[192,128]{1,0:T(8,128)S(1)} collective-permute-done((f32[192,128]{1,0:T(8,128)S(1)}, f32[192,128]{1,0:T(8,128)S(1)}, u32[]{:S(2)}, u32[]{:S(2)}) %collective-permute-start.12) | collective-permute-done | bytes 98336 | tf_op jit(solution)/shard_map/ppermute | solution.py:632
  91.9 11.6 %basis.4 = (f32[256,128]{1,0:T(8,128)}, f32[256,128]{1,0:T(8,128)}, f32[256,128]{1,0:T(8,128)}) custom-call(s32[4]{0:T(128)} %add_add_fusion.6.state_ref, f32[192,128]{1,0:T(8,128)} %copy-done.15, f32[192,128]{1,0:T(8,128)} %copy-done.25, f32[256,128]{1,0:T(8,128)} %broadcast_select_fusion.4.refs_0_, f32[256,256]{1,0:T(8,128)} %broadcast_select_fusion.3.refs_1_, ...), custom_call_target="tpu_custom_call" | custom-call | tf_op jit(solution)/shard_map/basis/pallas_call | solution.py:392
  103.5 14.6 %project.3 = (bf16[256,8192]{1,0:T(8,128)(2,1)}, bf16[256,8192]{1,0:T(8,128)(2,1)}, f32[192,128]{1,0:T(8,128)}, f32[192,128]{1,0:T(8,128)}, f32[128,2048]{1,0:T(...) custom-call(s32[4]{0:T(128)} %add_add_fusion.7.state_ref, f32[256,64,256]{2,1,0:T(8,128)} %bitcast.48, ...), custom_call_target="tpu_custom_call" | custom-call | tf_op jit(solution)/shard_map/project/pallas_call | solution.py:349
  122.0 2.1 collective-permute-start.21
  124.1 1.9 collective-permute-done.19
  129.7 9.9 %basis.5.front_ref.refs_4_ = f32[256,128]{1,0:T(8,128)} custom-call(s32[4]{0:T(128)} %add_add_fusion.7.state_ref, f32[192,128]{1,0:T(8,128)} %copy-done.13, f32[192,128]{1,0:T(8,128)} %copy-done.23, f32[256,128]{1,0:T(8,128)} %refs_0_.3), custom_call_target="tpu_custom_call" | custom-call | tf_op jit(solution)/shard_map/basis/pallas_call | solution.py:392
  139.6 3.6 %round_piece.7.refs_3_ = f32[128,2048]{1,0:T(8,128)} custom-call(s32[4]{0:T(128)} %copy-done.30, f32[256,128]{1,0:T(8,128)} %basis.5.front_ref.refs_4_, bf16[256,8192]{1,0:T(8,128)(2,1)} %get-tuple-element.102.high_ref, bf16[256,8192]{1,0:T(8,128)(2,1)} %get-tuple-element.103.low_ref), custom_call_target="tpu_custom_call" | custom-call | tf_op jit(solution)/shard_map/round_piece/pallas_call | solution.py:415
  143.2 5.4 %collective-permute-start.25 = (f32[128,2048]{1,0:T(8,128)}, f32[128,2048]{1,0:T(8,128)S(1)}, u32[]{:S(2)}, u32[]{:S(2)}) collective-permute-start(f32[128,2048]{1,0:T(8,128)} %round_piece.7.refs_3_), channel_id=1, source_target_pairs={{0,3},{1,2},{2,1},{3,0},{4,7},{5,6},{6,5},{7,4},{8,11},{9,10},{10,... | collective-permute-start | bytes 3145736 | tf_op jit(solution)/shard_map/ppermute | solution.py:641
  148.6 3.6 %round_piece.6.refs_2_ = f32[128,2048]{1,0:T(8,128)} custom-call(s32[4]{0:T(128)} %copy-done.29, f32[256,128]{1,0:T(8,128)} %basis.5.front_ref.refs_4_, bf16[256,8192]{1,0:T(8,128)(2,1)} %get-tuple-element.102.high_ref, bf16[256,8192]{1,0:T(8,128)(2,1)} %get-tuple-element.103.low_ref), custom_call_target="tpu_custom_call" | custom-call | tf_op jit(solution)/shard_map/round_piece/pallas_call | solution.py:415
  152.3 2.0 collective-permute-start.24
  154.3 3.6 %round_piece.5.refs_1_ = f32[128,2048]{1,0:T(8,128)} custom-call(s32[4]{0:T(128)} %copy-done.28, f32[256,128]{1,0:T(8,128)} %basis.5.front_ref.refs_4_, bf16[256,8192]{1,0:T(8,128)(2,1)} %get-tuple-element.102.high_ref, bf16[256,8192]{1,0:T(8,128)(2,1)} %get-tuple-element.103.low_ref), custom_call_target="tpu_custom_call" | custom-call | tf_op jit(solution)/shard_map/round_piece/pallas_call | solution.py:415
  157.9 2.8 collective-permute-start.23
  160.7 3.1 collective-permute-start.26
  163.8 4.8 %collective-permute-start.27 = (f32[256,128]{1,0:T(8,128)S(1)}, f32[256,128]{1,0:T(8,128)S(1)}, u32[]{:S(2)}, u32[]{:S(2)}) collective-permute-start(f32[256,128]{1,0:T(8,128)S(1)} %copy-done), channel_id=1, source_target_pairs={{0,2},{1,3},{2,0},{3,1},{4,6},{5,7},{6,4},{7,5},{8,10},{9,11},{10,... | collective-permute-start | bytes 393224 | tf_op jit(solution)/shard_map/ppermute | solution.py:641
  168.6 16.5 %collective-permute-done.26.refs_5_ = f32[256,128]{1,0:T(8,128)S(1)} collective-permute-done((f32[256,128]{1,0:T(8,128)S(1)}, f32[256,128]{1,0:T(8,128)S(1)}, u32[]{:S(2)}, u32[]{:S(2)}) %collective-permute-start.26) | collective-permute-done | bytes 131104 | tf_op jit(solution)/shard_map/ppermute | solution.py:641
  185.1 2.2 collective-permute-start.28
  187.8 3.6 %round_piece.4.refs_0_ = f32[128,2048]{1,0:T(8,128)} custom-call(s32[4]{0:T(128)} %copy-done.31, f32[256,128]{1,0:T(8,128)} %basis.5.front_ref.refs_4_, bf16[256,8192]{1,0:T(8,128)(2,1)} %get-tuple-element.102.high_ref, bf16[256,8192]{1,0:T(8,128)(2,1)} %get-tuple-element.103.low_ref), custom_call_target="tpu_custom_call" | custom-call | tf_op jit(solution)/shard_map/round_piece/pallas_call | solution.py:415
  191.5 7.5 %collective-permute-done.27.refs_6_ = f32[256,128]{1,0:T(8,128)S(1)} collective-permute-done((f32[256,128]{1,0:T(8,128)S(1)}, f32[256,128]{1,0:T(8,128)S(1)}, u32[]{:S(2)}, u32[]{:S(2)}) %collective-permute-start.27) | collective-permute-done | bytes 131104 | tf_op jit(solution)/shard_map/ppermute | solution.py:641
  200.0 12.2 %margin_terms.2 = (f32[4,160,128]{2,1,0:T(8,128)}, f32[4,160,128]{2,1,0:T(8,128)}) custom-call(s32[4]{0:T(128)} %add_add_fusion.7.state_ref, f32[128,2048]{1,0:T(8,128)} %round_piece.4.refs_0_, f32[128,2048]{1,0:T(8,128)} %collective-permute-done.23.refs_1_, f32[128,2048]{1,0:T(8,128)} %collective-permute-done.24.refs_2_, f32[128,2048]{1,0:T(8,128)} %copy-done.10, ...), custom_call_target="tpu_custom_call" | custom-call | tf_op jit(solution)/shard_map/margin_terms/pallas_call | solution.py:588
  212.2 1.8 collective-permute-done.29
  215.0 1.6 collective-permute-start.30
  223.2 2.1 collective-permute-start.33
  226.4 11.6 %collective-permute-done.33 = f32[160,128]{1,0:T(8,128)S(1)} collective-permute-done((f32[160,128]{1,0:T(8,128)S(1)}, f32[160,128]{1,0:T(8,128)S(1)}, u32[]{:S(2)}, u32[]{:S(2)}) %collective-permute-start.33) | collective-permute-done | bytes 81952 | tf_op jit(solution)/shard_map/ppermute | solution.py:632
  239.3 5.8 %collective-permute-done.35 = f32[160,128]{1,0:T(8,128)S(1)} collective-permute-done((f32[160,128]{1,0:T(8,128)S(1)}, f32[160,128]{1,0:T(8,128)S(1)}, u32[]{:S(2)}, u32[]{:S(2)}) %collective-permute-start.35) | collective-permute-done | bytes 81952 | tf_op jit(solution)/shard_map/ppermute | solution.py:632
  246.4 3.2 collective-permute-done.36
  250.8 4.1 %collective-permute-done.38 = f32[160,128]{1,0:T(8,128)S(1)} collective-permute-done((f32[160,128]{1,0:T(8,128)S(1)}, f32[160,128]{1,0:T(8,128)S(1)}, u32[]{:S(2)}, u32[]{:S(2)}) %collective-permute-start.38) | collective-permute-done | bytes 81952 | tf_op jit(solution)/shard_map/ppermute | solution.py:632
  255.0 29.6 %collective-permute-start.39 = (f32[4,160,128]{2,1,0:T(8,128)S(1)}, f32[4,160,128]{2,1,0:T(8,128)S(1)}, u32[]{:S(2)}, u32[]{:S(2)}) collective-permute-start(f32[4,160,128]{2,1,0:T(8,128)S(1)} %pad_maximum_fusion.refs_4_.refs_0_), channel_id=1, source_target_pairs={{0,16},{16,0},{1,17},{17,1},{2,18},{18,2},{3,19},{19,3},{4,20},{20... | collective-permute-start | bytes 983048 | tf_op jit(solution)/shard_map/ppermute | solution.py:632
  288.3 2.9 margin_terms.3
  291.2 8.1 %collective-permute-start.43 = (f32[4,160,128]{2,1,0:T(8,128)}, f32[4,160,128]{2,1,0:T(8,128)S(1)}, u32[]{:S(2)}, u32[]{:S(2)}) collective-permute-start(f32[4,160,128]{2,1,0:T(8,128)} %get-tuple-element.112), channel_id=1, source_target_pairs={{0,16},{16,0},{1,17},{17,1},{2,18},{18,2},{3,19},{19,3},{4,20},{20... | collective-permute-start | bytes 983048 | tf_op jit(solution)/shard_map/ppermute | solution.py:632
  300.8 1.6 collective-permute-start.44
  305.8 1.9 collective-permute-done.45
  307.7 2.0 collective-permute-done.46
  311.2 1.6 collective-permute-start.48
  314.2 6.3 %collective-permute-done.48 = f32[160,128]{1,0:T(8,128)S(1)} collective-permute-done((f32[160,128]{1,0:T(8,128)S(1)}, f32[160,128]{1,0:T(8,128)S(1)}, u32[]{:S(2)}, u32[]{:S(2)}) %collective-permute-start.48) | collective-permute-done | bytes 81952 | tf_op jit(solution)/shard_map/ppermute | solution.py:632
  322.1 1.9 collective-permute-start.52
  325.5 1.9 collective-permute-done.52
  327.6 5.2 %lay_out.1 = f32[128,4,16,128]{3,2,1,0:T(8,128)} custom-call(s32[4]{0:T(128)} %add_add_fusion.6.state_ref, f32[128,2048]{1,0:T(8,128)} %round_piece.4.refs_0_, f32[128,2048]{1,0:T(8,128)} %round_piece.5.refs_1_, f32[128,2048]{1,0:T(8,128)} %round_piece.6.refs_2_, f32[128,2048]{1,0:T(8,128)} %round_piece.7.refs_3_, ...), custom_call_target="tpu_custom_call" | custom-call | tf_op jit(solution)/shard_map/lay_out/pallas_call | solution.py:465
  334.3 2.2 pick.1
  (172 shorter events, 61.1 us)
Async XLA Ops:
  13.7 5.8 %collective-permute-start.1 = (f32[192,128]{1,0:T(8,128)S(1)}, f32[192,128]{1,0:T(8,128)S(1)}, u32[]{:S(2)}, u32[]{:S(2)}) collective-permute-start(f32[192,128]{1,0:T(8,128)S(1)} %broadcast_select_fusion.6), channel_id=1, source_target_pairs={{0,4},{4,0},{8,12},{12,8},{1,5},{5,1},{9,13},{13,9},{2,6},{6,2},{1... | collective-permute-start | bytes 294920 | tf_op jit(solution)/shard_map/ppermute | solution.py:632
  16.8 5.7 %collective-permute-start.2 = (f32[192,128]{1,0:T(8,128)S(1)}, f32[192,128]{1,0:T(8,128)S(1)}, u32[]{:S(2)}, u32[]{:S(2)}) collective-permute-start(f32[192,128]{1,0:T(8,128)S(1)} %broadcast_select_fusion.6), channel_id=1, source_target_pairs={{0,8},{4,12},{8,0},{12,4},{1,9},{5,13},{9,1},{13,5},{2,10},{6,14},... | collective-permute-start | bytes 294920 | tf_op jit(solution)/shard_map/ppermute | solution.py:632
  18.3 5.5 %collective-permute-start.3 = (f32[192,128]{1,0:T(8,128)S(1)}, f32[192,128]{1,0:T(8,128)S(1)}, u32[]{:S(2)}, u32[]{:S(2)}) collective-permute-start(f32[192,128]{1,0:T(8,128)S(1)} %broadcast_select_fusion.6), channel_id=1, source_target_pairs={{0,12},{4,8},{8,4},{12,0},{1,13},{5,9},{9,5},{13,1},{2,14},{6,10},... | collective-permute-start | bytes 294920 | tf_op jit(solution)/shard_map/ppermute | solution.py:632
  42.7 2.2 collective-permute-start.5
  44.9 5.5 %collective-permute-start.6 = (f32[192,128]{1,0:T(8,128)S(1)}, f32[192,128]{1,0:T(8,128)S(1)}, u32[]{:S(2)}, u32[]{:S(2)}) collective-permute-start(f32[192,128]{1,0:T(8,128)S(1)} %broadcast_select_fusion.8), channel_id=1, source_target_pairs={{0,4},{4,0},{8,12},{12,8},{1,5},{5,1},{9,13},{13,9},{2,6},{6,2},{1... | collective-permute-start | bytes 294920 | tf_op jit(solution)/shard_map/ppermute | solution.py:632
  45.5 7.8 %collective-permute-start.7 = (f32[192,128]{1,0:T(8,128)S(1)}, f32[192,128]{1,0:T(8,128)S(1)}, u32[]{:S(2)}, u32[]{:S(2)}) collective-permute-start(f32[192,128]{1,0:T(8,128)S(1)} %broadcast_select_fusion.8), channel_id=1, source_target_pairs={{0,8},{4,12},{8,0},{12,4},{1,9},{5,13},{9,1},{13,5},{2,10},{6,14},... | collective-permute-start | bytes 294920 | tf_op jit(solution)/shard_map/ppermute | solution.py:632
  46.0 7.3 %collective-permute-start.8 = (f32[192,128]{1,0:T(8,128)S(1)}, f32[192,128]{1,0:T(8,128)S(1)}, u32[]{:S(2)}, u32[]{:S(2)}) collective-permute-start(f32[192,128]{1,0:T(8,128)S(1)} %broadcast_select_fusion.8), channel_id=1, source_target_pairs={{0,12},{4,8},{8,4},{12,0},{1,13},{5,9},{9,5},{13,1},{2,14},{6,10},... | collective-permute-start | bytes 294920 | tf_op jit(solution)/shard_map/ppermute | solution.py:632
  48.4 30.9 %collective-permute-start.15 = (f32[256,128]{1,0:T(8,128)S(1)}, f32[256,128]{1,0:T(8,128)S(1)}, u32[]{:S(2)}, u32[]{:S(2)}) collective-permute-start(f32[256,128]{1,0:T(8,128)S(1)} %copy-done.11), channel_id=1, source_target_pairs={{0,16},{16,0},{1,17},{17,1},{2,18},{18,2},{3,19},{19,3},{4,20},{20... | collective-permute-start | bytes 393224 | tf_op jit(solution)/shard_map/ppermute | solution.py:632
  54.1 30.0 %collective-permute-start.17 = (f32[256,256]{1,0:T(8,128)}, f32[256,256]{1,0:T(8,128)S(1)}, u32[]{:S(2)}, u32[]{:S(2)}) collective-permute-start(f32[256,256]{1,0:T(8,128)} %get-tuple-element.89), channel_id=1, source_target_pairs={{0,16},{16,0},{1,17},{17,1},{2,18},{18,2},{3,19},{19,3},{4,20},{20... | collective-permute-start | bytes 786440 | tf_op jit(solution)/shard_map/ppermute | solution.py:632
  61.6 18.9 %collective-permute-start.10 = (f32[192,128]{1,0:T(8,128)}, f32[192,128]{1,0:T(8,128)S(1)}, u32[]{:S(2)}, u32[]{:S(2)}) collective-permute-start(f32[192,128]{1,0:T(8,128)} %get-tuple-element.87), channel_id=1, source_target_pairs={{0,16},{16,0},{1,17},{17,1},{2,18},{18,2},{3,19},{19,3},{4,20},{20... | collective-permute-start | bytes 294920 | tf_op jit(solution)/shard_map/ppermute | solution.py:632
  80.0 10.0 %collective-permute-start.16 = (f32[256,256]{1,0:T(8,128)S(1)}, f32[256,256]{1,0:T(8,128)S(1)}, u32[]{:S(2)}, u32[]{:S(2)}) collective-permute-start(f32[256,256]{1,0:T(8,128)S(1)} %copy-done.17), channel_id=1, source_target_pairs={{0,16},{16,0},{1,17},{17,1},{2,18},{18,2},{3,19},{19,3},{4,20},{20... | collective-permute-start | bytes 786440 | tf_op jit(solution)/shard_map/ppermute | solution.py:632
  80.5 5.5 %collective-permute-start.11 = (f32[192,128]{1,0:T(8,128)S(1)}, f32[192,128]{1,0:T(8,128)S(1)}, u32[]{:S(2)}, u32[]{:S(2)}) collective-permute-start(f32[192,128]{1,0:T(8,128)S(1)} %broadcast_select_fusion.7), channel_id=1, source_target_pairs={{0,4},{4,0},{8,12},{12,8},{1,5},{5,1},{9,13},{13,9},{2,6},{6,2},{1... | collective-permute-start | bytes 294920 | tf_op jit(solution)/shard_map/ppermute | solution.py:632
  82.1 7.8 %collective-permute-start.12 = (f32[192,128]{1,0:T(8,128)S(1)}, f32[192,128]{1,0:T(8,128)S(1)}, u32[]{:S(2)}, u32[]{:S(2)}) collective-permute-start(f32[192,128]{1,0:T(8,128)S(1)} %broadcast_select_fusion.7), channel_id=1, source_target_pairs={{0,8},{4,12},{8,0},{12,4},{1,9},{5,13},{9,1},{13,5},{2,10},{6,14},... | collective-permute-start | bytes 294920 | tf_op jit(solution)/shard_map/ppermute | solution.py:632
  82.6 7.2 %collective-permute-start.13 = (f32[192,128]{1,0:T(8,128)S(1)}, f32[192,128]{1,0:T(8,128)S(1)}, u32[]{:S(2)}, u32[]{:S(2)}) collective-permute-start(f32[192,128]{1,0:T(8,128)S(1)} %broadcast_select_fusion.7), channel_id=1, source_target_pairs={{0,12},{4,8},{8,4},{12,0},{1,13},{5,9},{9,5},{13,1},{2,14},{6,10},... | collective-permute-start | bytes 294920 | tf_op jit(solution)/shard_map/ppermute | solution.py:632
  120.6 5.5 %collective-permute-start.19 = (f32[192,128]{1,0:T(8,128)S(1)}, f32[192,128]{1,0:T(8,128)S(1)}, u32[]{:S(2)}, u32[]{:S(2)}) collective-permute-start(f32[192,128]{1,0:T(8,128)S(1)} %broadcast_select_fusion.5), channel_id=1, source_target_pairs={{0,4},{4,0},{8,12},{12,8},{1,5},{5,1},{9,13},{13,9},{2,6},{6,2},{1... | collective-permute-start | bytes 294920 | tf_op jit(solution)/shard_map/ppermute | solution.py:632
  121.2 5.4 %collective-permute-start.20 = (f32[192,128]{1,0:T(8,128)S(1)}, f32[192,128]{1,0:T(8,128)S(1)}, u32[]{:S(2)}, u32[]{:S(2)}) collective-permute-start(f32[192,128]{1,0:T(8,128)S(1)} %broadcast_select_fusion.5), channel_id=1, source_target_pairs={{0,8},{4,12},{8,0},{12,4},{1,9},{5,13},{9,1},{13,5},{2,10},{6,14},... | collective-permute-start | bytes 294920 | tf_op jit(solution)/shard_map/ppermute | solution.py:632
  122.0 5.6 %collective-permute-start.21 = (f32[192,128]{1,0:T(8,128)S(1)}, f32[192,128]{1,0:T(8,128)S(1)}, u32[]{:S(2)}, u32[]{:S(2)}) collective-permute-start(f32[192,128]{1,0:T(8,128)S(1)} %broadcast_select_fusion.5), channel_id=1, source_target_pairs={{0,12},{4,8},{8,4},{12,0},{1,13},{5,9},{9,5},{13,1},{2,14},{6,10},... | collective-permute-start | bytes 294920 | tf_op jit(solution)/shard_map/ppermute | solution.py:632
  143.2 55.8 %collective-permute-start.25 = (f32[128,2048]{1,0:T(8,128)}, f32[128,2048]{1,0:T(8,128)S(1)}, u32[]{:S(2)}, u32[]{:S(2)}) collective-permute-start(f32[128,2048]{1,0:T(8,128)} %round_piece.7.refs_3_), channel_id=1, source_target_pairs={{0,3},{1,2},{2,1},{3,0},{4,7},{5,6},{6,5},{7,4},{8,11},{9,10},{10,... | collective-permute-start | bytes 3145736 | tf_op jit(solution)/shard_map/ppermute | solution.py:641
  152.3 46.7 %collective-permute-start.24 = (f32[128,2048]{1,0:T(8,128)}, f32[128,2048]{1,0:T(8,128)}, u32[]{:S(2)}, u32[]{:S(2)}) collective-permute-start(f32[128,2048]{1,0:T(8,128)} %round_piece.6.refs_2_), channel_id=1, source_target_pairs={{0,2},{1,3},{2,0},{3,1},{4,6},{5,7},{6,4},{7,5},{8,10},{9,11},{10,... | collective-permute-start | bytes 3145736 | tf_op jit(solution)/shard_map/ppermute | solution.py:641
  157.9 41.1 %collective-permute-start.23 = (f32[128,2048]{1,0:T(8,128)}, f32[128,2048]{1,0:T(8,128)}, u32[]{:S(2)}, u32[]{:S(2)}) collective-permute-start(f32[128,2048]{1,0:T(8,128)} %round_piece.5.refs_1_), channel_id=1, source_target_pairs={{0,1},{1,0},{2,3},{3,2},{4,5},{5,4},{6,7},{7,6},{8,9},{9,8},{10,11... | collective-permute-start | bytes 3145736 | tf_op jit(solution)/shard_map/ppermute | solution.py:641
  160.7 24.4 %collective-permute-start.26 = (f32[256,128]{1,0:T(8,128)S(1)}, f32[256,128]{1,0:T(8,128)S(1)}, u32[]{:S(2)}, u32[]{:S(2)}) collective-permute-start(f32[256,128]{1,0:T(8,128)S(1)} %copy-done), channel_id=1, source_target_pairs={{0,1},{1,0},{2,3},{3,2},{4,5},{5,4},{6,7},{7,6},{8,9},{9,8},{10,11... | collective-permute-start | bytes 393224 | tf_op jit(solution)/shard_map/ppermute | solution.py:641
  163.8 35.2 %collective-permute-start.27 = (f32[256,128]{1,0:T(8,128)S(1)}, f32[256,128]{1,0:T(8,128)S(1)}, u32[]{:S(2)}, u32[]{:S(2)}) collective-permute-start(f32[256,128]{1,0:T(8,128)S(1)} %copy-done), channel_id=1, source_target_pairs={{0,2},{1,3},{2,0},{3,1},{4,6},{5,7},{6,4},{7,5},{8,10},{9,11},{10,... | collective-permute-start | bytes 393224 | tf_op jit(solution)/shard_map/ppermute | solution.py:641
  185.1 13.9 %collective-permute-start.28 = (f32[256,128]{1,0:T(8,128)S(1)}, f32[256,128]{1,0:T(8,128)}, u32[]{:S(2)}, u32[]{:S(2)}) collective-permute-start(f32[256,128]{1,0:T(8,128)S(1)} %copy-done), channel_id=1, source_target_pairs={{0,3},{1,2},{2,1},{3,0},{4,7},{5,6},{6,5},{7,4},{8,11},{9,10},{10,... | collective-permute-start | bytes 393224 | tf_op jit(solution)/shard_map/ppermute | solution.py:641
  212.2 1.8 collective-permute-start.29
  215.0 5.0 %collective-permute-start.30 = (f32[160,128]{1,0:T(8,128)S(1)}, f32[160,128]{1,0:T(8,128)S(1)}, u32[]{:S(2)}, u32[]{:S(2)}) collective-permute-start(f32[160,128]{1,0:T(8,128)S(1)} %get-tuple-element.118), channel_id=1, source_target_pairs={{0,4},{4,0},{8,12},{12,8},{1,5},{5,1},{9,13},{13,9},{2,6},{6,2},{1... | collective-permute-start | bytes 245768 | tf_op jit(solution)/shard_map/ppermute | solution.py:632
  216.7 5.2 %collective-permute-start.31 = (f32[160,128]{1,0:T(8,128)S(1)}, f32[160,128]{1,0:T(8,128)S(1)}, u32[]{:S(2)}, u32[]{:S(2)}) collective-permute-start(f32[160,128]{1,0:T(8,128)S(1)} %get-tuple-element.117), channel_id=1, source_target_pairs={{0,8},{4,12},{8,0},{12,4},{1,9},{5,13},{9,1},{13,5},{2,10},{6,14},... | collective-permute-start | bytes 245768 | tf_op jit(solution)/shard_map/ppermute | solution.py:632
  217.8 5.3 %collective-permute-start.32 = (f32[160,128]{1,0:T(8,128)S(1)}, f32[160,128]{1,0:T(8,128)S(1)}, u32[]{:S(2)}, u32[]{:S(2)}) collective-permute-start(f32[160,128]{1,0:T(8,128)S(1)} %get-tuple-element.116), channel_id=1, source_target_pairs={{0,12},{4,8},{8,4},{12,0},{1,13},{5,9},{9,5},{13,1},{2,14},{6,10},... | collective-permute-start | bytes 245768 | tf_op jit(solution)/shard_map/ppermute | solution.py:632
  218.6 66.0 %collective-permute-start.40 = (f32[128,2048]{1,0:T(8,128)S(1)}, f32[128,2048]{1,0:T(8,128)S(1)}, u32[]{:S(2)}, u32[]{:S(2)}) collective-permute-start(f32[128,2048]{1,0:T(8,128)S(1)} %copy-done.5), channel_id=1, source_target_pairs={{16,17},{17,16},{18,19},{19,18},{20,21},{21,20},{22,23},{23,22},{2... | collective-permute-start | bytes 3145736 | tf_op jit(solution)/shard_map/ppermute | solution.py:641
  219.3 65.3 %collective-permute-start.41 = (f32[128,2048]{1,0:T(8,128)S(1)}, f32[128,2048]{1,0:T(8,128)S(1)}, u32[]{:S(2)}, u32[]{:S(2)}) collective-permute-start(f32[128,2048]{1,0:T(8,128)S(1)} %copy-done.6), channel_id=1, source_target_pairs={{16,18},{17,19},{18,16},{19,17},{20,22},{21,23},{22,20},{23,21},{2... | collective-permute-start | bytes 3145736 | tf_op jit(solution)/shard_map/ppermute | solution.py:641
  220.1 65.5 %collective-permute-start.42 = (f32[128,2048]{1,0:T(8,128)}, f32[128,2048]{1,0:T(8,128)S(1)}, u32[]{:S(2)}, u32[]{:S(2)}) collective-permute-start(f32[128,2048]{1,0:T(8,128)} %get-tuple-element.107.refs_7_), channel_id=1, source_target_pairs={{16,19},{17,18},{18,17},{19,16},{20,23},{21,22},{22,21},{23,20},{2... | collective-permute-start | bytes 3145736 | tf_op jit(solution)/shard_map/ppermute | solution.py:641
  223.2 14.7 %collective-permute-start.33 = (f32[160,128]{1,0:T(8,128)S(1)}, f32[160,128]{1,0:T(8,128)S(1)}, u32[]{:S(2)}, u32[]{:S(2)}) collective-permute-start(f32[160,128]{1,0:T(8,128)S(1)} %fusion.3), channel_id=1, source_target_pairs={{0,1},{1,0},{2,3},{3,2},{4,5},{5,4},{6,7},{7,6},{8,9},{9,8},{10,11... | collective-permute-start | bytes 245768 | tf_op jit(solution)/shard_map/ppermute | solution.py:632
  225.3 14.0 %collective-permute-start.34 = (f32[160,128]{1,0:T(8,128)S(1)}, f32[160,128]{1,0:T(8,128)S(1)}, u32[]{:S(2)}, u32[]{:S(2)}) collective-permute-start(f32[160,128]{1,0:T(8,128)S(1)} %fusion.3), channel_id=1, source_target_pairs={{0,2},{1,3},{2,0},{3,1},{4,6},{5,7},{6,4},{7,5},{8,10},{9,11},{10,... | collective-permute-start | bytes 245768 | tf_op jit(solution)/shard_map/ppermute | solution.py:632
  237.9 7.2 %collective-permute-start.35 = (f32[160,128]{1,0:T(8,128)S(1)}, f32[160,128]{1,0:T(8,128)S(1)}, u32[]{:S(2)}, u32[]{:S(2)}) collective-permute-start(f32[160,128]{1,0:T(8,128)S(1)} %fusion.3), channel_id=1, source_target_pairs={{0,3},{1,2},{2,1},{3,0},{4,7},{5,6},{6,5},{7,4},{8,11},{9,10},{10,... | collective-permute-start | bytes 245768 | tf_op jit(solution)/shard_map/ppermute | solution.py:632
  245.1 4.5 %collective-permute-start.36 = (f32[160,128]{1,0:T(8,128)S(1)}, f32[160,128]{1,0:T(8,128)S(1)}, u32[]{:S(2)}, u32[]{:S(2)}) collective-permute-start(f32[160,128]{1,0:T(8,128)S(1)} %add_add_fusion.5), channel_id=1, source_target_pairs={{0,4},{4,0},{8,12},{12,8},{1,5},{5,1},{9,13},{13,9},{2,6},{6,2},{1... | collective-permute-start | bytes 245768 | tf_op jit(solution)/shard_map/ppermute | solution.py:632
  246.4 4.4 %collective-permute-start.37 = (f32[160,128]{1,0:T(8,128)S(1)}, f32[160,128]{1,0:T(8,128)S(1)}, u32[]{:S(2)}, u32[]{:S(2)}) collective-permute-start(f32[160,128]{1,0:T(8,128)S(1)} %add_add_fusion.5), channel_id=1, source_target_pairs={{0,8},{4,12},{8,0},{12,4},{1,9},{5,13},{9,1},{13,5},{2,10},{6,14},... | collective-permute-start | bytes 245768 | tf_op jit(solution)/shard_map/ppermute | solution.py:632
  249.6 5.3 %collective-permute-start.38 = (f32[160,128]{1,0:T(8,128)S(1)}, f32[160,128]{1,0:T(8,128)S(1)}, u32[]{:S(2)}, u32[]{:S(2)}) collective-permute-start(f32[160,128]{1,0:T(8,128)S(1)} %add_add_fusion.5), channel_id=1, source_target_pairs={{0,12},{4,8},{8,4},{12,0},{1,13},{5,9},{9,5},{13,1},{2,14},{6,10},... | collective-permute-start | bytes 245768 | tf_op jit(solution)/shard_map/ppermute | solution.py:632
  255.0 32.5 %collective-permute-start.39 = (f32[4,160,128]{2,1,0:T(8,128)S(1)}, f32[4,160,128]{2,1,0:T(8,128)S(1)}, u32[]{:S(2)}, u32[]{:S(2)}) collective-permute-start(f32[4,160,128]{2,1,0:T(8,128)S(1)} %pad_maximum_fusion.refs_4_.refs_0_), channel_id=1, source_target_pairs={{0,16},{16,0},{1,17},{17,1},{2,18},{18,2},{3,19},{19,3},{4,20},{20... | collective-permute-start | bytes 983048 | tf_op jit(solution)/shard_map/ppermute | solution.py:632
  291.2 9.5 %collective-permute-start.43 = (f32[4,160,128]{2,1,0:T(8,128)}, f32[4,160,128]{2,1,0:T(8,128)S(1)}, u32[]{:S(2)}, u32[]{:S(2)}) collective-permute-start(f32[4,160,128]{2,1,0:T(8,128)} %get-tuple-element.112), channel_id=1, source_target_pairs={{0,16},{16,0},{1,17},{17,1},{2,18},{18,2},{3,19},{19,3},{4,20},{20... | collective-permute-start | bytes 983048 | tf_op jit(solution)/shard_map/ppermute | solution.py:632
  300.8 5.0 %collective-permute-start.44 = (f32[160,128]{1,0:T(8,128)S(1)}, f32[160,128]{1,0:T(8,128)S(1)}, u32[]{:S(2)}, u32[]{:S(2)}) collective-permute-start(f32[160,128]{1,0:T(8,128)S(1)} %get-tuple-element.115), channel_id=1, source_target_pairs={{0,4},{4,0},{8,12},{12,8},{1,5},{5,1},{9,13},{13,9},{2,6},{6,2},{1... | collective-permute-start | bytes 245768 | tf_op jit(solution)/shard_map/ppermute | solution.py:632
  302.4 5.2 %collective-permute-start.45 = (f32[160,128]{1,0:T(8,128)S(1)}, f32[160,128]{1,0:T(8,128)S(1)}, u32[]{:S(2)}, u32[]{:S(2)}) collective-permute-start(f32[160,128]{1,0:T(8,128)S(1)} %get-tuple-element.114), channel_id=1, source_target_pairs={{0,8},{4,12},{8,0},{12,4},{1,9},{5,13},{9,1},{13,5},{2,10},{6,14},... | collective-permute-start | bytes 245768 | tf_op jit(solution)/shard_map/ppermute | solution.py:632
  303.6 6.0 %collective-permute-start.46 = (f32[160,128]{1,0:T(8,128)S(1)}, f32[160,128]{1,0:T(8,128)S(1)}, u32[]{:S(2)}, u32[]{:S(2)}) collective-permute-start(f32[160,128]{1,0:T(8,128)S(1)} %get-tuple-element.113), channel_id=1, source_target_pairs={{0,12},{4,8},{8,4},{12,0},{1,13},{5,9},{9,5},{13,1},{2,14},{6,10},... | collective-permute-start | bytes 245768 | tf_op jit(solution)/shard_map/ppermute | solution.py:632
  309.7 4.5 %collective-permute-start.47 = (f32[160,128]{1,0:T(8,128)S(1)}, f32[160,128]{1,0:T(8,128)S(1)}, u32[]{:S(2)}, u32[]{:S(2)}) collective-permute-start(f32[160,128]{1,0:T(8,128)S(1)} %fusion.1), channel_id=1, source_target_pairs={{0,1},{1,0},{2,3},{3,2},{4,5},{5,4},{6,7},{7,6},{8,9},{9,8},{10,11... | collective-permute-start | bytes 245768 | tf_op jit(solution)/shard_map/ppermute | solution.py:632
  311.2 9.3 %collective-permute-start.48 = (f32[160,128]{1,0:T(8,128)S(1)}, f32[160,128]{1,0:T(8,128)S(1)}, u32[]{:S(2)}, u32[]{:S(2)}) collective-permute-start(f32[160,128]{1,0:T(8,128)S(1)} %fusion.1), channel_id=1, source_target_pairs={{0,2},{1,3},{2,0},{3,1},{4,6},{5,7},{6,4},{7,5},{8,10},{9,11},{10,... | collective-permute-start | bytes 245768 | tf_op jit(solution)/shard_map/ppermute | solution.py:632
  312.7 7.7 %collective-permute-start.49 = (f32[160,128]{1,0:T(8,128)S(1)}, f32[160,128]{1,0:T(8,128)S(1)}, u32[]{:S(2)}, u32[]{:S(2)}) collective-permute-start(f32[160,128]{1,0:T(8,128)S(1)} %fusion.1), channel_id=1, source_target_pairs={{0,3},{1,2},{2,1},{3,0},{4,7},{5,6},{6,5},{7,4},{8,11},{9,10},{10,... | collective-permute-start | bytes 245768 | tf_op jit(solution)/shard_map/ppermute | solution.py:632
  320.5 4.5 %collective-permute-start.50 = (f32[160,128]{1,0:T(8,128)S(1)}, f32[160,128]{1,0:T(8,128)S(1)}, u32[]{:S(2)}, u32[]{:S(2)}) collective-permute-start(f32[160,128]{1,0:T(8,128)S(1)} %add_add_fusion.4), channel_id=1, source_target_pairs={{0,4},{4,0},{8,12},{12,8},{1,5},{5,1},{9,13},{13,9},{2,6},{6,2},{1... | collective-permute-start | bytes 245768 | tf_op jit(solution)/shard_map/ppermute | solution.py:632
  321.1 4.4 %collective-permute-start.51 = (f32[160,128]{1,0:T(8,128)S(1)}, f32[160,128]{1,0:T(8,128)S(1)}, u32[]{:S(2)}, u32[]{:S(2)}) collective-permute-start(f32[160,128]{1,0:T(8,128)S(1)} %add_add_fusion.4), channel_id=1, source_target_pairs={{0,8},{4,12},{8,0},{12,4},{1,9},{5,13},{9,1},{13,5},{2,10},{6,14},... | collective-permute-start | bytes 245768 | tf_op jit(solution)/shard_map/ppermute | solution.py:632
  322.1 5.3 %collective-permute-start.52 = (f32[160,128]{1,0:T(8,128)S(1)}, f32[160,128]{1,0:T(8,128)S(1)}, u32[]{:S(2)}, u32[]{:S(2)}) collective-permute-start(f32[160,128]{1,0:T(8,128)S(1)} %add_add_fusion.4), channel_id=1, source_target_pairs={{0,12},{4,8},{8,4},{12,0},{1,13},{5,9},{9,5},{13,1},{2,14},{6,10},... | collective-permute-start | bytes 245768 | tf_op jit(solution)/shard_map/ppermute | solution.py:632
  327.5 6.0 %collective-permute-start.53 = (f32[4,160,128]{2,1,0:T(8,128)S(1)}, f32[4,160,128]{2,1,0:T(8,128)S(1)}, u32[]{:S(2)}, u32[]{:S(2)}) collective-permute-start(f32[4,160,128]{2,1,0:T(8,128)S(1)} %pad_maximum_fusion.1.refs_2_), channel_id=1, source_target_pairs={{0,16},{16,0},{1,17},{17,1},{2,18},{18,2},{3,19},{19,3},{4,20},{20... | collective-permute-start | bytes 983048 | tf_op jit(solution)/shard_map/ppermute | solution.py:632
  (38 other events, 317.1 us)
where the time goes:
time: 337 us; the launch traced here: 336 us
  starting transfers between devices  117 us (35%)
  Pallas kernels  106 us (31%)
  waiting for transfers between devices  95.1 us (28%)
  local copies, waits for them, and re-layouts  8.6 us (3%)
  other arithmetic  7.83 us (2%)
    ppermute x45, starting transfers between devices, send(): return lax.ppermute(block, axis, [(i, i ^ distance) for i in range(size)])  94.7 us
    ppermute x45, waiting for transfers between devices, send(): return lax.ppermute(block, axis, [(i, i ^ distance) for i in range(size)])  71.2 us
    ppermute x9, waiting for transfers between devices, send_from(): return lax.ppermute(block, ('cores', 'vec'), pairs)  24 us
    pallas_call x3, Pallas kernels, basis(): pl.pallas_call(functools.partial(basis_body, absorbed), in_specs=[SMEM] +...  23.4 us
    ppermute x9, starting transfers between devices, send_from(): return lax.ppermute(block, ('cores', 'vec'), pairs)  22.8 us
    pallas_call x2, Pallas kernels, project(): pl.pallas_call(functools.partial(project_body, pieces), grid_spec=pltpu.P...  19.1 us
    pallas_call x1, Pallas kernels, absorbed_gram(): pl.pallas_call(absorbed_body, grid_spec=pltpu.PrefetchScalarGridSpec(num_...  16.8 us
    pallas_call x2, Pallas kernels, margin_terms(): pl.pallas_call(functools.partial(margin_body, count, first), grid_spec=pl...  15.1 us
  transfers between devices with their start and end apart: 54, of which 37 were waited for; matrix products, arithmetic and copies ran while one was open for 1% of the time, Pallas kernels for 7%

commit v1 on v0

--- a/solution.py
+++ b/solution.py
@@ -12,7 +12,6 @@
 MODE = 256
 F32 = jnp.float32
 BF16 = jnp.bfloat16
-BASIS_UNROLL = 2
 
 
 def contract(left, right, left_dim, right_dim, precision=None):
@@ -48,36 +47,52 @@
     return pl.BlockSpec(dims, lambda *_: (0,) * len(dims))
 
 
-def inverse_factor(gram, out_ref, unroll=1):
+def inverse_factor(gram, out_ref, unrolled=False):
     size = gram.shape[0]
     row_id = lax.broadcasted_iota(jnp.int32, (size, size), 0)
     col_id = lax.broadcasted_iota(jnp.int32, (size, size), 1)
     inverse = jnp.where(row_id == col_id, 1.0, 0.0).astype(F32)
+
+    def eliminate(gram, inverse, column, open_rows):
+        left = gram.shape[0]
+        rows = row_id[:left]
+        columns = [
+            jnp.broadcast_to(gram[:, column + t : column + t + 1], (left, size)) for t in range(8)
+        ]
+        scale = jnp.zeros((8, size), F32)
+        for t in range(8):
+            pivot = columns[t][t : t + 1, :]
+            use = rows > t
+            if open_rows is not None:
+                use = use & open_rows
+            factor = jnp.where(use, columns[t] * (1.0 / pivot), 0.0)
+            for s in range(t + 1, 8):
+                columns[s] = columns[s] - factor * columns[s][t : t + 1, :]
+            gram = gram - factor * gram[t : t + 1, :]
+            inverse = inverse - factor * inverse[t : t + 1, :]
+            scale = jnp.where(rows[:8] == t, lax.rsqrt(pivot), scale)
+        return gram, inverse, inverse[:8] * scale
+
+    if unrolled:
+        for start in range(0, size, 8):
+            gram, inverse, rows = eliminate(gram, inverse, start, None)
+            out_ref[start : start + 8, :] = rows
+            gram, inverse = gram[8:], inverse[8:]
+        return
+
     done = 0
     while done < size:
         left = size - done
-        panels = left // 16 if left > 16 * unroll else left // 8
-        rows = row_id[:left]
-
-        def panel(k, carry, left=left, done=done, rows=rows):
+        panels = left // 16 if left > 16 else left // 8
+
+        def panel(k, carry, left=left, done=done):
             gram, inverse = carry
-            open_rows = rows < left - 8 * k
-            columns = [jnp.broadcast_to(gram[:, t : t + 1], (left, size)) for t in range(8)]
-            scale = jnp.zeros((8, size), F32)
-            for t in range(8):
-                pivot = columns[t][t : t + 1, :]
-                factor = jnp.where((rows > t) & open_rows, columns[t] * (1.0 / pivot), 0.0)
-                for s in range(t + 1, 8):
-                    columns[s] = columns[s] - factor * columns[s][t : t + 1, :]
-                gram = gram - factor * gram[t : t + 1, :]
-                inverse = inverse - factor * inverse[t : t + 1, :]
-                scale = jnp.where(rows[:8] == t, lax.rsqrt(pivot), scale)
-            out_ref[pl.ds(pl.multiple_of(done + 8 * k, 8), 8), :] = inverse[:8] * scale
+            gram, inverse, rows = eliminate(gram, inverse, 0, row_id[:left] < left - 8 * k)
+            out_ref[pl.ds(pl.multiple_of(done + 8 * k, 8), 8), :] = rows
             gram = pltpu.roll(jnp.concatenate([gram[8:], gram[:8]], axis=0), size - 8, 1)
             return gram, jnp.concatenate([inverse[8:], inverse[:8]], axis=0)
 
-        carry = (gram[:left], inverse[:left])
-        gram, inverse = lax.fori_loop(0, panels, panel, carry, unroll=min(unroll, panels))
+        gram, inverse = lax.fori_loop(0, panels, panel, (gram[:left], inverse[:left]))
         done += 8 * panels
         gram, inverse = gram[: size - done], inverse[: size - done]
 
@@ -88,8 +103,10 @@
     first = jnp.concatenate([value[:half, :half], value[half : half + cut, :half]], axis=0)
     second = jnp.concatenate([value[half + cut :, :half], value[half:, half:]], axis=0)
     mine = state_ref[2] == 0
-    keep_ref[...] = jnp.where(mine, first, second)
-    give_ref[...] = jnp.where(mine, second, first)
+    keep = jnp.where(mine, first, second)
+    give = jnp.where(mine, second, first)
+    keep_ref[...] = keep
+    give_ref[...] = give
 
 
 def read_halves(state_ref, own_ref, other_ref):
@@ -112,7 +129,7 @@
 
 
 def half_dims(rank):
-    return (3 * rank // 4, rank // 2)
+    return [(3 * rank // 4, rank // 2)] * 2
 
 
 def gram_body(state_ref, core_ref, keep_ref, give_ref, acc_ref):
@@ -148,10 +165,10 @@
             num_scalar_prefetch=1,
             grid=(mode_count // modes,),
             in_specs=[core_spec(rank, modes, width)],
-            out_specs=[fixed(*half_dims(width))] * 2,
+            out_specs=[fixed(*dims) for dims in half_dims(width)],
             scratch_shapes=[pltpu.VMEM((width, 2 * width), F32)],
         ),
-        out_shape=[shape(half_dims(width))] * 2,
+        out_shape=[shape(dims) for dims in half_dims(width)],
         name="gram",
     )(state, core)
 
@@ -159,21 +176,37 @@
 def write_factor(state_ref, own_ref, other_ref, low_ref, inv_ref, work_ref):
     half = low_ref.shape[0] // 2
     first, cross, second = read_halves(state_ref, own_ref, other_ref)
-    inverse_factor(first, work_ref)
-    inv_first = work_ref[...]
-    low_cross = exact(cross, inv_first, 1, 1)
-    second = second - exact(low_cross, low_cross, 1, 1)
-    inverse_factor(second, work_ref)
-    inv_second = work_ref[...]
-    zero = jnp.zeros((half, half), F32)
-    low_ref[:half, :half] = exact(first, inv_first, 1, 1)
-    low_ref[:half, half:] = zero
-    low_ref[half:, :half] = low_cross
-    low_ref[half:, half:] = exact(second, inv_second, 1, 1)
-    inv_ref[:half, :half] = inv_first
-    inv_ref[:half, half:] = zero
-    inv_ref[half:, :half] = -exact(inv_second, exact(low_cross, inv_first, 1, 0), 1, 0)
-    inv_ref[half:, half:] = inv_second
+    low_ref[:half, :half] = first
+    low_ref[half:, :half] = cross
+    low_ref[half:, half:] = second
+    low_ref[:half, half:] = jnp.zeros((half, half), F32)
+    inv_ref[:half, half:] = jnp.zeros((half, half), F32)
+
+    def block(k, _):
+        here = pl.ds(pl.multiple_of(k * half, half), half)
+        diagonal = jnp.where(k == 0, low_ref[:half, :half], low_ref[half:, half:])
+        inverse_factor(diagonal, work_ref)
+        inverse = work_ref[...]
+        inv_ref[here, :half] = inverse
+        lower = exact(diagonal, inverse, 1, 1)
+
+        @pl.when(k == 0)
+        def _():
+            low_ref[:half, :half] = lower
+            low_cross = exact(low_ref[half:, :half], inverse, 1, 1)
+            low_ref[half:, :half] = low_cross
+            low_ref[half:, half:] -= exact(low_cross, low_cross, 1, 1)
+
+        @pl.when(k == 1)
+        def _():
+            low_ref[half:, half:] = lower
+            inv_ref[half:, half:] = inverse
+            across = exact(low_ref[half:, :half], inv_ref[:half, :half], 1, 0)
+            inv_ref[half:, :half] = -exact(inverse, across, 1, 0)
+
+        return 0
+
+    lax.fori_loop(0, 2, block, 0)
 
 
 def absorbed_body(
@@ -234,8 +267,8 @@
         grid_spec=pltpu.PrefetchScalarGridSpec(
             num_scalar_prefetch=1,
             grid=(mode_count // modes,),
-            in_specs=[fixed(*half_dims(rank))] * 2 + [core_spec(rank, modes, width)],
-            out_specs=[fixed(*half_dims(width))] * 2 + [fixed(rank, rank)] * 2,
+            in_specs=[fixed(*dims) for dims in half_dims(rank)] + [core_spec(rank, modes, width)],
+            out_specs=[fixed(*dims) for dims in half_dims(width)] + [fixed(rank, rank)] * 2,
             scratch_shapes=[
                 pltpu.VMEM((2 * rank, rank), BF16),
                 pltpu.VMEM((width, 2 * width), F32),
@@ -243,12 +276,12 @@
                 pltpu.VMEM((rank // 2, rank // 2), F32),
             ],
         ),
-        out_shape=[shape(half_dims(width))] * 2 + [shape((rank, rank))] * 2,
+        out_shape=[shape(dims) for dims in half_dims(width)] + [shape((rank, rank))] * 2,
         name="absorbed_gram",
     )(state, *outer, core)
 
 
-def project_step(state_ref, core_ref, map_ref, high_ref, low_ref, keep_ref, give_ref, both_ref, acc_ref):
+def project_step(state_ref, core_ref, map_ref, high_ref, low_ref, half_refs, both_ref, acc_ref):
     step = pl.program_id(0)
     rank, modes, width = core_ref.shape
     kept = map_ref.shape[1]
@@ -276,7 +309,7 @@
     def _():
         cross = acc_ref[:, rank:]
         total = acc_ref[:, :rank] + (cross + cross.T)
-        write_halves(state_ref, total, keep_ref, give_ref)
+        write_halves(state_ref, total, *half_refs)
 
 
 def shaped_piece(front_ref, high_ref, low_ref):
@@ -288,18 +321,18 @@
     return first[:kept] + (first[kept:] + second)
 
 
-def project_body(pieces, state_ref, *refs):
+def project_body(pieces, halves, state_ref, *refs):
     core_ref, map_ref, refs = refs[0], refs[1], refs[2:]
     if pieces:
         other_refs, refs = refs[:3], refs[3:]
-        piece_refs, slots_ref, copied = refs[4 : 4 + pieces], refs[-2], refs[-1]
-    high_ref, low_ref, keep_ref, give_ref = refs[:4]
-    both_ref, acc_ref = refs[4 + pieces : 6 + pieces]
+        piece_refs, slots_ref, copied = refs[2 + halves : 2 + halves + pieces], refs[-2], refs[-1]
+    high_ref, low_ref, half_refs = refs[0], refs[1], refs[2 : 2 + halves]
+    both_ref, acc_ref = refs[2 + halves + pieces : 4 + halves + pieces]
 
     @pl.when(state_ref[0] == 1)
     def _():
         project_step(
-            state_ref, core_ref, map_ref, high_ref, low_ref, keep_ref, give_ref, both_ref, acc_ref
+            state_ref, core_ref, map_ref, high_ref, low_ref, half_refs, both_ref, acc_ref
         )
 
     if pieces:
@@ -330,8 +363,9 @@
     modes = mode_count // pieces if pieces else min(16, mode_count)
     wide = pl.BlockSpec((rank, modes * kept), lambda s, state: (0, s * state[0]))
     in_specs = [core_spec(rank, modes, width), fixed(width, kept)]
-    out_specs = [wide, wide] + [fixed(*half_dims(rank))] * 2
-    out_shape = [shape((rank, mode_count * kept), BF16)] * 2 + [shape(half_dims(rank))] * 2
+    half_shapes = half_dims(rank)
+    out_specs = [wide, wide] + [fixed(*dims) for dims in half_shapes]
+    out_shape = [shape((rank, mode_count * kept), BF16)] * 2 + [shape(d) for d in half_shapes]
     scratch = [pltpu.VMEM((width, 2 * kept), BF16), pltpu.VMEM((rank, 2 * rank), F32)]
     operands = [core, right_map]
     if pieces:
@@ -347,7 +381,7 @@
             pltpu.SemaphoreType.DMA((pieces,)),
         ]
     return pl.pallas_call(
-        functools.partial(project_body, pieces),
+        functools.partial(project_body, pieces, len(half_shapes)),
         grid_spec=pltpu.PrefetchScalarGridSpec(
             num_scalar_prefetch=1,
             grid=(mode_count // modes,),
@@ -362,40 +396,75 @@
 
 SMEM = pl.BlockSpec(memory_space=pltpu.SMEM)
 VMEM = pl.BlockSpec(memory_space=pltpu.VMEM)
-
-
-def basis_body(absorbed, state_ref, own_ref, other_ref, *refs):
-    if absorbed:
-        sketch_ref, low_ref, inv_ref, basis_ref, front_ref, map_ref, work_ref = refs
-    else:
-        sketch_ref, basis_ref, work_ref = refs
+ANY = pl.BlockSpec(memory_space=pl.ANY)
+
+
+def basis_body(
+    state_ref,
+    own_ref,
+    other_ref,
+    sketch_ref,
+    low_any,
+    inv_any,
+    basis_ref,
+    front_ref,
+    map_ref,
+    work_ref,
+    total_ref,
+    low_ref,
+    inv_ref,
+    copied,
+):
+    absorbed = state_ref[4] == 1
 
     @pl.when(state_ref[0] == 1)
     def _():
-        total = whole(read_halves(state_ref, own_ref, other_ref))
-        if absorbed:
+        copies = [
+            pltpu.make_async_copy(low_any, low_ref, copied.at[0]),
+            pltpu.make_async_copy(inv_any, inv_ref, copied.at[1]),
+        ]
+
+        @pl.when(absorbed)
+        def _():
+            for copy in copies:
+                copy.start()
+
+        total_ref[...] = whole(read_halves(state_ref, own_ref, other_ref))
+
+        @pl.when(absorbed)
+        def _():
+            for copy in copies:
+                copy.wait()
             lower = low_ref[...]
-            total = exact(exact(lower, total, 0, 0), lower, 1, 0)
+            total_ref[...] = exact(exact(lower, total_ref[...], 0, 0), lower, 1, 0)
+
+        total = total_ref[...]
         powered = exact(total, exact(total, sketch_ref[...], 1, 0), 1, 0)
-        inverse_factor(exact(powered, powered, 0, 0), work_ref, BASIS_UNROLL)
+        inverse_factor(exact(powered, powered, 0, 0), work_ref)
         frame = exact(powered, work_ref[...], 1, 1)
         basis_ref[...] = frame
-        if absorbed:
-            front_ref[...] = exact(lower, frame, 1, 0)
+
+        @pl.when(absorbed)
+        def _():
+            front_ref[...] = exact(low_ref[...], frame, 1, 0)
             map_ref[...] = exact(inv_ref[...], frame, 0, 0)
 
 
-def basis(state, halves, sketch, lower=None, inverse=None):
-    absorbed = lower is not None
-    operands = (*halves, sketch) + ((lower, inverse) if absorbed else ())
-    kept = sketch.shape[1]
-    return pl.pallas_call(
-        functools.partial(basis_body, absorbed),
-        in_specs=[SMEM] + [VMEM] * len(operands),
-        out_shape=[shape(sketch.shape)] * (3 if absorbed else 1),
-        scratch_shapes=[pltpu.VMEM((kept, kept), F32)],
+def basis(state, halves, sketch, lower, inverse):
+    rank, kept = sketch.shape
+    return pl.pallas_call(
+        basis_body,
+        in_specs=[SMEM] + [VMEM] * 3 + [ANY] * 2,
+        out_shape=[shape(sketch.shape)] * 3,
+        scratch_shapes=[
+            pltpu.VMEM((kept, kept), F32),
+            pltpu.VMEM((rank, rank), F32),
+            pltpu.VMEM((rank, rank), F32),
+            pltpu.VMEM((rank, rank), F32),
+            pltpu.SemaphoreType.DMA((2,)),
+        ],
         name="basis",
-    )(state, *operands)
+    )(state, *halves, sketch, lower, inverse)
 
 
 def piece_body(state_ref, front_ref, high_ref, low_ref, piece_ref):
@@ -481,22 +550,29 @@
     return [(p, q) for p in range(count) for q in range(p, count)]
 
 
+def chunk_rows(state_ref, half, d, chunks, kept):
+    size = kept // (2 * chunks)
+    start = (half * chunks + (state_ref[3] ^ d)) * size
+    return (pl.multiple_of(start, 8) if size % 8 == 0 else start), size
+
+
+def halves_of(state_ref, own_ref, other_ref):
+    return (own_ref, state_ref[2]), (other_ref, 1 - state_ref[2])
+
+
 def place_chunks(state_ref, own_ref, other_ref, out_ref):
-    chunks, size = own_ref.shape[:2]
-    side, row = state_ref[2], state_ref[3]
+    chunks, rows, kept = own_ref.shape
     for d in range(chunks):
-        for ref, half in ((own_ref, side), (other_ref, 1 - side)):
-            start = pl.multiple_of((half * chunks + (row ^ d)) * size, 8)
-            out_ref[pl.ds(start, size), :] = ref[d]
-
-
-def margin_body(count, first, state_ref, *refs):
-    piece_refs, refs = refs[:count], refs[count:]
-    if first:
-        frame_refs, refs = refs[:count], refs[count:]
-        keep_ref, give_ref, stage_ref, env_ref, out_ref, frame_stage_ref = refs
-    else:
-        own_ref, other_ref, keep_ref, give_ref, stage_ref, env_ref, out_ref, env_in_ref = refs
+        for ref, half in halves_of(state_ref, own_ref, other_ref):
+            start, size = chunk_rows(state_ref, half, d, chunks, kept)
+            for i in range(rows // size):
+                out_ref[pl.ds(i * kept + start, size), :] = ref[d, i * size : (i + 1) * size, :]
+
+
+def margin_body(count, state_ref, *refs):
+    piece_refs, frame_anys, refs = refs[:count], refs[count : 2 * count], refs[2 * count :]
+    own_any, other_any, _, keep_ref, give_ref, stage_ref, env_ref, out_ref = refs[:8]
+    frame_ref, env_own_ref, env_other_ref, env_in_ref, copied = refs[8:]
     step = pl.program_id(0)
     pairs = pair_list(count)
     index_of = {pair: i for i, pair in enumerate(pairs)}
@@ -509,16 +585,34 @@
         @pl.when(step == 0)
         def _():
             out_ref[...] = jnp.zeros_like(out_ref)
-            if first:
-                for d in range(count):
-                    frame_stage_ref[me ^ d] = frame_refs[d][...]
-            else:
-                place_chunks(state_ref, own_ref, other_ref, env_in_ref)
+
+            @pl.when(state_ref[4] == 0)
+            def _():
+                copies = [
+                    pltpu.make_async_copy(frame_anys[d], frame_ref.at[me ^ d], copied.at[d])
+                    for d in range(count)
+                ]
+                for copy in copies:
+                    copy.start()
+                for copy in copies:
+                    copy.wait()
+                for i, (p, q) in enumerate(pairs):
+                    env_in_ref[i * kept : (i + 1) * kept] = exact(frame_ref[p], frame_ref[q], 0, 0)
+
+            @pl.when(state_ref[4] == 1)
+            def _():
+                copies = [
+                    pltpu.make_async_copy(own_any, env_own_ref, copied.at[0]),
+                    pltpu.make_async_copy(other_any, env_other_ref, copied.at[1]),
+                ]
+                for copy in copies:
+                    copy.start()
+                for copy in copies:
+                    copy.wait()
+                place_chunks(state_ref, env_own_ref, env_other_ref, env_in_ref)
+
             for i, (p, q) in enumerate(pairs):
-                if first:
-                    env = exact(frame_stage_ref[p], frame_stage_ref[q], 0, 0)
-                else:
-                    env = env_in_ref[i * kept : (i + 1) * kept]
+                env = env_in_ref[i * kept : (i + 1) * kept]
                 env_high, env_low = split(env)
                 env_ref[q, p * kept : (p + 1) * kept] = env_high
                 env_ref[q, (count + p) * kept : (count + p + 1) * kept] = env_low
@@ -562,59 +656,100 @@
 
         @pl.when(step == pl.num_programs(0) - 1)
         def _():
-            chunks, size = keep_ref.shape[:2]
-            side, row = state_ref[2], state_ref[3]
+            chunks, rows = keep_ref.shape[:2]
             for d in range(chunks):
-                for ref, half in ((keep_ref, side), (give_ref, 1 - side)):
-                    start = pl.multiple_of((half * chunks + (row ^ d)) * size, 8)
-                    ref[d] = out_ref[pl.ds(start, size), :]
-
-
-def margin_terms(state, pieces, rows, frames=None, env=None):
+                for ref, half in halves_of(state_ref, keep_ref, give_ref):
+                    start, size = chunk_rows(state_ref, half, d, chunks, kept)
+                    for i in range(rows // size):
+                        ref[d, i * size : (i + 1) * size, :] = out_ref[
+                            pl.ds(i * kept + start, size), :
+                        ]
+
+
+def margin_terms(state, pieces, frames, env, token):
     count = len(pieces)
     kept, wide = pieces[0].shape
     chunk = min(4 * kept, wide)
-    first = frames is not None
     total = count * (count + 1) // 2 * kept
     piece_spec = pl.BlockSpec((kept, chunk), lambda s, state: (0, s * state[0]))
-    extra = list(frames) if first else list(env)
-    part = (rows, total // (2 * rows), kept)
+    part = env[0].shape
     scratch = [
         pltpu.VMEM((count, kept, chunk), F32),
         pltpu.VMEM((count, 2 * count * kept, kept), BF16),
         pltpu.VMEM((total, kept), F32),
-        pltpu.VMEM((count, *frames[0].shape) if first else (total, kept), F32),
+        pltpu.VMEM((count, *frames[0].shape), F32),
+        pltpu.VMEM(part, F32),
+        pltpu.VMEM(part, F32),
+        pltpu.VMEM((total, kept), F32),
+        pltpu.SemaphoreType.DMA((count,)),
     ]
     return pl.pallas_call(
-        functools.partial(margin_body, count, first),
+        functools.partial(margin_body, count),
         grid_spec=pltpu.PrefetchScalarGridSpec(
             num_scalar_prefetch=1,
             grid=(wide // chunk,),
-            in_specs=[piece_spec] * count + [fixed(*x.shape) for x in extra],
+            in_specs=[piece_spec] * count + [ANY] * (count + 3),
             out_specs=[fixed(*part)] * 2,
             scratch_shapes=scratch,
         ),
         out_shape=[shape(part)] * 2,
         name="margin_terms",
-    )(state, *pieces, *extra)
-
-
-def pick_body(count, state_ref, *refs):
-    out_ref, env_ref = refs[4:]
+    )(state, *pieces, *frames, *env, token)
+
+
+def unset(dims):
+    return pl.pallas_call(
+        lambda ref: None, out_specs=ANY, out_shape=shape(dims), name="unset"
+    )()
+
+
+def pair_index(count, first, second):
+    low, high = jnp.minimum(first, second), jnp.maximum(first, second)
+    return low * count - low * (low - 1) // 2 + high - low
+
+
+def owner_body(count, state_ref, *refs):
+    part_refs, (out_ref, sum_ref) = refs[:-2], refs[-2:]
+    sum_ref[...] = tree_sum([ref[...] for ref in part_refs])
+    size = sum_ref.shape[0] // (count * (count + 1) // 2)
+    for d in range(count):
+        for q in range(count):
+            start = pair_index(count, state_ref[1] ^ d, q) * size
+            if size % 8 == 0:
+                start = pl.multiple_of(start, 8)
+            out_ref[d, q * size : (q + 1) * size, :] = sum_ref[pl.ds(start, size), :]
+
+
+def owner_rows(state, parts, count):
+    rows, kept = parts[0].shape
+    size = rows // (count * (count + 1) // 2)
+    return pl.pallas_call(
+        functools.partial(owner_body, count),
+        in_specs=[SMEM] + [VMEM] * len(parts),
+        out_shape=shape((count, count * size, kept)),
+        scratch_shapes=[pltpu.VMEM((rows, kept), F32)],
+        name="owner_rows",
+    )(state, *parts)
+
+
+def pick_body(count, state_ref, own_ref, other_ref, own_row_ref, other_row_ref, out_ref, env_ref):
     kept = out_ref.shape[0]
     me = state_ref[1]
-    for side in (0, 1):
-
-        @pl.when(state_ref[2] == side)
-        def _(side=side):
-            place_chunks(state_ref, refs[2 * side], refs[2 * side + 1], env_ref)
-
-    for q in range(count):
-        low, high = jnp.minimum(me, q), jnp.maximum(me, q)
-        index = low * count - low * (low - 1) // 2 + high - low
-        block = env_ref[pl.ds(pl.multiple_of(index * kept, kept), kept), :]
-        block = jnp.where(me > q, block.T, block)
-        out_ref[:, q * kept : (q + 1) * kept] = block
+
+    @pl.when(state_ref[2] == 0)
+    def _():
+        place_chunks(state_ref, own_ref, other_ref, env_ref)
+        for q in range(count):
+            start = pl.multiple_of(pair_index(count, me, q) * kept, kept)
+            block = env_ref[pl.ds(start, kept), :]
+            out_ref[:, q * kept : (q + 1) * kept] = jnp.where(me > q, block.T, block)
+
+    @pl.when(state_ref[2] == 1)
+    def _():
+        place_chunks(state_ref, own_row_ref, other_row_ref, env_ref)
+        for q in range(count):
+            block = env_ref[q * kept : (q + 1) * kept, :]
+            out_ref[:, q * kept : (q + 1) * kept] = jnp.where(me > q, block.T, block)
 
 
 def pick(state, env_first, env_last, count):
@@ -655,9 +790,11 @@
     row = lax.axis_index("row")
     vec = lax.axis_index("vec")
     first_side = (side == 0).astype(jnp.int32)
-    state_first = jnp.stack([first_side, vec, side, row])
-    state_last = jnp.stack([1 - first_side, vec, side, row])
-    state_both = jnp.stack([jnp.int32(1), vec, side, row])
+    place = [vec, side, row]
+    state_first = jnp.stack([first_side, *place, jnp.int32(0)])
+    state_last = jnp.stack([1 - first_side, *place, jnp.int32(0)])
+    state_next = jnp.stack([1 - first_side, *place, jnp.int32(1)])
+    state_both = jnp.stack([jnp.int32(1), *place, jnp.int32(1)])
     scale = math.sqrt(kept * MODE)
 
     def row_total(keep, give, holder):
@@ -665,28 +802,38 @@
         own = exchange_sum(mine, "row", row_size)
         return own, swap(own)
 
-    def env_total(keep, give, holder):
+    def row_parts(keep, give, holder):
         mine = jnp.where(side == holder, keep, swap(give))
-        parts = [mine[0]] + [send(mine[d], "row", row_size, d) for d in range(1, row_size)]
-        chunk = exchange_sum(tree_sum(parts), "vec", vec_size)
+        return [mine[0]] + [send(mine[d], "row", row_size, d) for d in range(1, row_size)]
+
+    def row_collect(chunk):
         own = jnp.stack([chunk] + [send(chunk, "row", row_size, d) for d in range(1, row_size)])
         return own, swap(own)
 
+    def env_total(keep, give, holder):
+        return row_collect(exchange_sum(tree_sum(row_parts(keep, give, holder)), "vec", vec_size))
+
+    def env_rows(keep, give, holder):
+        rows = owner_rows(state_both, row_parts(keep, give, holder), vec_size)
+        parts = [rows[0]] + [send(rows[d], "vec", vec_size, d) for d in range(1, vec_size)]
+        return row_collect(tree_sum(parts))
+
     def at(state, d):
         return state.at[1].set(vec ^ d)
 
-    def sent(pieces, holder):
-        out = [pieces[0]]
-        for d in range(1, vec_size):
-            out.append(send_from(pieces[d], holder, vec_size, d))
-        return out
-
+    def sent(pieces, holder, distances):
+        for d in distances:
+            pieces[d] = send_from(pieces[d], holder, vec_size, d)
+
+    late = [vec_size // 2]
+    pair_count = vec_size * (vec_size + 1) // 2
+    blank = unset((row_size, pair_count * kept // (2 * row_size), kept))
     gram_first = row_total(*gram(state_first, core), 0)
-    *gram_last, lower, inverse = absorbed_gram(state_last, gram_first, core)
+    *gram_last, lower_own, inverse_own = absorbed_gram(state_last, gram_first, core)
     gram_last = row_total(*gram_last, 1)
-    lower = jnp.where(side == 0, lower, swap(lower))
-    inverse = jnp.where(side == 0, inverse, swap(inverse))
-    (exit_frame,) = basis(state_last, gram_last, exit_sketch)
+    lower = jnp.where(side == 0, lower_own, swap(lower_own))
+    inverse = jnp.where(side == 0, inverse_own, swap(inverse_own))
+    exit_frame, _, _ = basis(state_last, gram_last, exit_sketch, lower_own, inverse_own)
     last_high, last_low, *left_last = project(state_last, core, exit_frame)
     left_last = row_total(*left_last, 1)
     other_sketch = swap(sketch)
@@ -706,16 +853,25 @@
         ]
     left_first = row_total(*left_first, 0)
     *own_last, left_own, left_other = lax.optimization_barrier((*own_last, *left_first))
-    pieces_last = sent(own_last, 1)
-    (frame_first,) = basis(state_first, (left_own, left_other), sketch)
+    left_first = (left_own, left_other)
+    pieces_last = list(own_last)
+    sent(pieces_last, 1, [d for d in range(1, vec_size) if d not in late])
+    frame_first, _, _ = basis(state_first, left_first, sketch, lower, inverse)
     own_first = [None] * vec_size
     for d in range(vec_size - 1, -1, -1):
         own_first[d] = round_piece(at(state_first, d), frame_first, first_high, first_low, vec_size)
-    pieces_first = sent(own_first, 0)
+    pieces_first = list(own_first)
+    sent(pieces_first, 0, range(1, vec_size))
     rounded = lay_out(state_both, own_first, own_last, scale)
     frames = [frame_first] + [send_from(frame_first, 0, vec_size, d) for d in range(1, vec_size)]
-    env_first = env_total(*margin_terms(state_first, pieces_first, row_size, frames=frames), 0)
-    env_last = env_total(*margin_terms(state_last, pieces_last, row_size, env=env_first), 1)
+    held = [pieces_last[d] for d in late]
+    token = swap(pieces_first[late[0]][:8, :128])
+    for d, piece in zip(late, held):
+        pieces_last[d] = piece
+    sent(pieces_last, 1, late)
+    env_first = margin_terms(state_first, pieces_first, frames, (blank, blank), token)
+    env_first = env_total(*env_first, 0)
+    env_last = env_rows(*margin_terms(state_next, pieces_last, frames, env_first, token), 1)
     margins = pick(state_both, env_first, env_last, vec_size)
     bases = jnp.where(side == 0, frame_first, frame_last) * math.sqrt(rank)
     return rounded.reshape(1, kept, mode_count, kept), bases[None], margins[None]

time: 337 us -> 339 us (level)
  waiting for transfers between devices: 95.1 us -> 84.8 us
  starting transfers between devices: 117 us -> 126 us
    ppermute x45 -> x46, waiting for transfers between devices: 71.2 us -> 60.8 us  [send(): return lax.ppermute(block, axis, [(i, i ^ distance) for i in range(size)])]
    ppermute x9, starting transfers between devices: 22.8 us -> 27.5 us  [send_from(): return lax.ppermute(block, ('cores', 'vec'), pairs)]
    ppermute x45 -> x46, starting transfers between devices: 94.7 us -> 98.5 us  [send(): return lax.ppermute(block, axis, [(i, i ^ distance) for i in range(size)])]
    pallas_call x7 -> x9, Pallas kernels: 57.6 us -> 60.2 us  [the longest x3 23.6 us: basis(): pl.pallas_call(basis_body, in_specs=[SMEM] + [VMEM] * 3 + [ANY] * 2, out_...]
    unnamed x68 -> x70, local copies, waits for them, and re-layouts: 8.49 us -> 6.81 us
  transfers between devices with their start and end apart: 54 -> 55, of which waited for: 37 -> 33; matrix products, arithmetic and copies ran while one was open for 1% -> 1% of each run, Pallas kernels for 7% -> 7%
where the time goes in v1:
time: 339 us; the launch traced here: 338 us
  starting transfers between devices  126 us (37%)
  Pallas kernels  109 us (32%)
  waiting for transfers between devices  84.8 us (25%)
  local copies, waits for them, and re-layouts  10.9 us (3%)
  other arithmetic  6.66 us (2%)
    ppermute x46, starting transfers between devices, send(): return lax.ppermute(block, axis, [(i, i ^ distance) for i in range(size)])  98.5 us
    ppermute x46, waiting for transfers between devices, send(): return lax.ppermute(block, axis, [(i, i ^ distance) for i in range(size)])  60.8 us
    ppermute x9, starting transfers between devices, send_from(): return lax.ppermute(block, ('cores', 'vec'), pairs)  27.5 us
    ppermute x9, waiting for transfers between devices, send_from(): return lax.ppermute(block, ('cores', 'vec'), pairs)  24 us
    pallas_call x3, Pallas kernels, basis(): pl.pallas_call(basis_body, in_specs=[SMEM] + [VMEM] * 3 + [ANY] * 2, out_...  23.6 us
    pallas_call x2, Pallas kernels, project(): pl.pallas_call(functools.partial(project_body, pieces, len(half_shapes)),...  18.9 us
    pallas_call x1, Pallas kernels, absorbed_gram(): pl.pallas_call(absorbed_body, grid_spec=pltpu.PrefetchScalarGridSpec(num_...  17.1 us
    pallas_call x2, Pallas kernels, margin_terms(): pl.pallas_call(functools.partial(margin_body, count), grid_spec=pltpu.Pre...  15.8 us
  transfers between devices with their start and end apart: 55, of which 33 were waited for; matrix products, arithmetic and copies ran while one was open for 1% of the time, Pallas kernels for 7%

profile of v1, /device:TPU:0, one launch (start us, length us, event | category | flops | bytes accessed | tf_op | source)
XLA Modules:
  0.0 338.3 jit_solution(1022938950779610795)
XLA Ops:
  1.3 10.1 %gram.1 = (f32[192,128]{1,0:T(8,128)}, f32[192,128]{1,0:T(8,128)}) custom-call(s32[5]{0:T(128)} %stack.72.state_ref, f32[256,64,256]{2,1,0:T(8,128)} %bitcast.53), custom_call_target="tpu_custom_call" | custom-call | tf_op jit(solution)/shard_map/gram/pallas_call | solution.py:162
  13.8 3.0 collective-permute-start.1
  19.6 2.9 collective-permute-done.2
  25.9 17.1 %absorbed_gram.1 = (f32[192,128]{1,0:T(8,128)}, f32[192,128]{1,0:T(8,128)}, f32[256,256]{1,0:T(8,128)}, f32[256,256]{1,0:T(8,128)}) custom-call(s32[5]{0:T(128)} %stack.74.state_ref, f32[192,128]{1,0:T(8,128)} %copy-done.13, f32[192,128]{1,0:T(8,128)} %copy-done.19, f32[256,64,256]{2,1,0:T(8,128)} %bitcast.54), custom_call_target="tpu_custom_call" | custom-call | tf_op jit(solution)/shard_map/absorbed_gram/pallas_call | solution.py:265
  46.0 2.5 collective-permute-start.8
  50.4 2.9 collective-permute-done.7
  55.3 1.9 basis.3
  57.3 4.4 %project.2 = (bf16[256,8192]{1,0:T(8,128)(2,1)}, bf16[256,8192]{1,0:T(8,128)(2,1)}, f32[192,128]{1,0:T(8,128)}, f32[192,128]{1,0:T(8,128)}) custom-call(s32[5]{0:T(128)} %stack.74.state_ref, f32[256,64,256]{2,1,0:T(8,128)} %bitcast.55, f32[256,128]{1,0:T(8,128)} %get-tuple-element.90.refs_1_), custom_call_target="tpu_custom_call" | custom-call | tf_op jit(solution)/shard_map/project/pallas_call | solution.py:383
  61.7 17.4 %collective-permute-start.10 = (f32[192,128]{1,0:T(8,128)}, f32[192,128]{1,0:T(8,128)S(1)}, u32[]{:S(2)}, u32[]{:S(2)}) collective-permute-start(f32[192,128]{1,0:T(8,128)} %get-tuple-element.92), channel_id=1, source_target_pairs={{0,16},{16,0},{1,17},{17,1},{2,18},{18,2},{3,19},{19,3},{4,20},{20... | collective-permute-start | bytes 294920 | tf_op jit(solution)/shard_map/ppermute | solution.py:767
  85.7 3.9 %collective-permute-done.12 = f32[192,128]{1,0:T(8,128)S(1)} collective-permute-done((f32[192,128]{1,0:T(8,128)S(1)}, f32[192,128]{1,0:T(8,128)S(1)}, u32[]{:S(2)}, u32[]{:S(2)}) %collective-permute-start.12) | collective-permute-done | bytes 98336 | tf_op jit(solution)/shard_map/ppermute | solution.py:767
  91.7 12.0 %basis.4 = (f32[256,128]{1,0:T(8,128)}, f32[256,128]{1,0:T(8,128)}, f32[256,128]{1,0:T(8,128)}) custom-call(s32[5]{0:T(128)} %stack.70.state_ref, f32[192,128]{1,0:T(8,128)} %copy-done.15, f32[192,128]{1,0:T(8,128)} %copy-done.21, f32[256,128]{1,0:T(8,128)} %broadcast_select_fusion.4.sketch_ref, f32[256,256]{1,0:T(8,128)} %broadcast_select_fusion.3.low_any, ...), custom_call_target="tpu_custom_call" | custom-call | tf_op jit(solution)/shard_map/basis/pallas_call | solution.py:455
  103.7 14.5 %project.3 = (bf16[256,8192]{1,0:T(8,128)(2,1)}, bf16[256,8192]{1,0:T(8,128)(2,1)}, f32[192,128]{1,0:T(8,128)}, f32[192,128]{1,0:T(8,128)}, f32[128,2048]{1,0:T(...) custom-call(s32[5]{0:T(128)} %stack.72.state_ref, f32[256,64,256]{2,1,0:T(8,128)} %bitcast.56, ...), custom_call_target="tpu_custom_call" | custom-call | tf_op jit(solution)/shard_map/project/pallas_call | solution.py:383
  122.2 2.2 collective-permute-start.21
  124.3 1.9 collective-permute-done.19
  129.8 9.7 %basis.5 = (f32[256,128]{1,0:T(8,128)}, f32[256,128]{1,0:T(8,128)}, f32[256,128]{1,0:T(8,128)}) custom-call(s32[5]{0:T(128)} %stack.72.state_ref, f32[192,128]{1,0:T(8,128)} %copy-done.14, f32[192,128]{1,0:T(8,128)} %copy-done.20, f32[256,128]{1,0:T(8,128)} %sketch_ref.3, f32[256,256]{1,0:T(8,128)} %broadcast_select_fusion.3.low_any, ...), custom_call_target="tpu_custom_call" | custom-call | tf_op jit(solution)/shard_map/basis/pallas_call | solution.py:455
  139.5 3.6 %round_piece.6.refs_2_ = f32[128,2048]{1,0:T(8,128)} custom-call(s32[5]{0:T(128)} %copy-done.31, f32[256,128]{1,0:T(8,128)} %get-tuple-element.105.front_ref.refs_4_, bf16[256,8192]{1,0:T(8,128)(2,1)} %get-tuple-element.106.high_ref, bf16[256,8192]{1,0:T(8,128)(2,1)} %get-tuple-element.107.low_ref), custom_call_target="tpu_custom_call" | custom-call | tf_op jit(solution)/shard_map/round_piece/pallas_call | solution.py:484
  143.1 4.4 %collective-permute-start.24 = (f32[128,2048]{1,0:T(8,128)}, f32[128,2048]{1,0:T(8,128)S(1)}, u32[]{:S(2)}, u32[]{:S(2)}) collective-permute-start(f32[128,2048]{1,0:T(8,128)} %round_piece.6.refs_2_), channel_id=1, source_target_pairs={{0,2},{1,3},{2,0},{3,1},{4,6},{5,7},{6,4},{7,5},{8,10},{9,11},{10,... | collective-permute-start | bytes 3145736 | tf_op jit(solution)/shard_map/ppermute | solution.py:776
  148.1 3.6 %round_piece.7.refs_3_ = f32[128,2048]{1,0:T(8,128)} custom-call(s32[5]{0:T(128)} %copy-done.30, f32[256,128]{1,0:T(8,128)} %get-tuple-element.105.front_ref.refs_4_, bf16[256,8192]{1,0:T(8,128)(2,1)} %get-tuple-element.106.high_ref, bf16[256,8192]{1,0:T(8,128)(2,1)} %get-tuple-element.107.low_ref), custom_call_target="tpu_custom_call" | custom-call | tf_op jit(solution)/shard_map/round_piece/pallas_call | solution.py:484
  151.6 3.3 collective-permute-start.25
  155.0 3.6 %round_piece.5.refs_1_ = f32[128,2048]{1,0:T(8,128)} custom-call(s32[5]{0:T(128)} %copy-done.29, f32[256,128]{1,0:T(8,128)} %get-tuple-element.105.front_ref.refs_4_, bf16[256,8192]{1,0:T(8,128)(2,1)} %get-tuple-element.106.high_ref, bf16[256,8192]{1,0:T(8,128)(2,1)} %get-tuple-element.107.low_ref), custom_call_target="tpu_custom_call" | custom-call | tf_op jit(solution)/shard_map/round_piece/pallas_call | solution.py:484
  158.6 2.2 collective-permute-start.23
  160.7 3.7 %collective-permute-start.26 = (f32[256,128]{1,0:T(8,128)S(1)}, f32[256,128]{1,0:T(8,128)S(1)}, u32[]{:S(2)}, u32[]{:S(2)}) collective-permute-start(f32[256,128]{1,0:T(8,128)S(1)} %copy-done), channel_id=1, source_target_pairs={{0,1},{1,0},{2,3},{3,2},{4,5},{5,4},{6,7},{7,6},{8,9},{9,8},{10,11... | collective-permute-start | bytes 393224 | tf_op jit(solution)/shard_map/ppermute | solution.py:776
  164.4 3.6 %collective-permute-start.27 = (f32[256,128]{1,0:T(8,128)S(1)}, f32[256,128]{1,0:T(8,128)S(1)}, u32[]{:S(2)}, u32[]{:S(2)}) collective-permute-start(f32[256,128]{1,0:T(8,128)S(1)} %copy-done), channel_id=1, source_target_pairs={{0,2},{1,3},{2,0},{3,1},{4,6},{5,7},{6,4},{7,5},{8,10},{9,11},{10,... | collective-permute-start | bytes 393224 | tf_op jit(solution)/shard_map/ppermute | solution.py:776
  168.0 15.4 %collective-permute-done.24.refs_2_ = f32[128,2048]{1,0:T(8,128)S(1)} collective-permute-done((f32[128,2048]{1,0:T(8,128)}, f32[128,2048]{1,0:T(8,128)S(1)}, u32[]{:S(2)}, u32[]{:S(2)}) %collective-permute-start.24) | collective-permute-done | bytes 1048608 | tf_op jit(solution)/shard_map/ppermute | solution.py:776
  183.4 5.3 %collective-permute-start.28 = (f32[256,128]{1,0:T(8,128)S(1)}, f32[256,128]{1,0:T(8,128)}, u32[]{:S(2)}, u32[]{:S(2)}) collective-permute-start(f32[256,128]{1,0:T(8,128)S(1)} %copy-done), channel_id=1, source_target_pairs={{0,3},{1,2},{2,1},{3,0},{4,7},{5,6},{6,5},{7,4},{8,11},{9,10},{10,... | collective-permute-start | bytes 393224 | tf_op jit(solution)/shard_map/ppermute | solution.py:776
  188.8 8.6 %collective-permute-done.26.refs_5_ = f32[256,128]{1,0:T(8,128)S(1)} collective-permute-done((f32[256,128]{1,0:T(8,128)S(1)}, f32[256,128]{1,0:T(8,128)S(1)}, u32[]{:S(2)}, u32[]{:S(2)}) %collective-permute-start.26) | collective-permute-done | bytes 131104 | tf_op jit(solution)/shard_map/ppermute | solution.py:776
  197.9 3.6 %round_piece.4.refs_0_ = f32[128,2048]{1,0:T(8,128)} custom-call(s32[5]{0:T(128)} %copy-done.32, f32[256,128]{1,0:T(8,128)} %get-tuple-element.105.front_ref.refs_4_, bf16[256,8192]{1,0:T(8,128)(2,1)} %get-tuple-element.106.high_ref, bf16[256,8192]{1,0:T(8,128)(2,1)} %get-tuple-element.107.low_ref), custom_call_target="tpu_custom_call" | custom-call | tf_op jit(solution)/shard_map/round_piece/pallas_call | solution.py:484
  202.7 13.0 %margin_terms.2 = (f32[4,160,128]{2,1,0:T(8,128)}, f32[4,160,128]{2,1,0:T(8,128)}) custom-call(s32[5]{0:T(128)} %stack.72.state_ref, f32[128,2048]{1,0:T(8,128)} %round_piece.4.refs_0_, f32[128,2048]{1,0:T(8,128)} %collective-permute-done.23.refs_1_, f32[128,2048]{1,0:T(8,128)} %copy-done.4, f32[128,2048]{1,0:T(8,128)} %collective-permute-done.25.refs_3_, ...), custom_call_target="tpu_custom_call" | custom-call | tf_op jit(solution)/shard_map/margin_terms/pallas_call | solution.py:686
  215.8 1.8 collective-permute-done.30
  222.3 1.6 collective-permute-start.41
  223.9 1.6 collective-permute-start.42
  225.5 1.6 collective-permute-start.43
  227.3 4.0 %collective-permute-start.35 = (f32[160,128]{1,0:T(8,128)S(1)}, f32[160,128]{1,0:T(8,128)S(1)}, u32[]{:S(2)}, u32[]{:S(2)}) collective-permute-start(f32[160,128]{1,0:T(8,128)S(1)} %fusion.1), channel_id=1, source_target_pairs={{0,2},{1,3},{2,0},{3,1},{4,6},{5,7},{6,4},{7,5},{8,10},{9,11},{10,... | collective-permute-start | bytes 245768 | tf_op jit(solution)/shard_map/ppermute | solution.py:767
  231.3 9.5 %collective-permute-done.34 = f32[160,128]{1,0:T(8,128)S(1)} collective-permute-done((f32[160,128]{1,0:T(8,128)S(1)}, f32[160,128]{1,0:T(8,128)S(1)}, u32[]{:S(2)}, u32[]{:S(2)}) %collective-permute-start.34) | collective-permute-done | bytes 81952 | tf_op jit(solution)/shard_map/ppermute | solution.py:767
  241.2 6.8 %collective-permute-done.36 = f32[160,128]{1,0:T(8,128)S(1)} collective-permute-done((f32[160,128]{1,0:T(8,128)S(1)}, f32[160,128]{1,0:T(8,128)S(1)}, u32[]{:S(2)}, u32[]{:S(2)}) %collective-permute-start.36) | collective-permute-done | bytes 81952 | tf_op jit(solution)/shard_map/ppermute | solution.py:767
  250.7 1.8 collective-permute-done.37
  252.5 2.1 collective-permute-start.39
  254.6 3.2 collective-permute-done.39
  257.9 29.7 %collective-permute-start.40 = (f32[4,160,128]{2,1,0:T(8,128)S(1)}, f32[4,160,128]{2,1,0:T(8,128)S(1)}, u32[]{:S(2)}, u32[]{:S(2)}) collective-permute-start(f32[4,160,128]{2,1,0:T(8,128)S(1)} %pad_maximum_fusion.refs_8_.own_ref), channel_id=1, source_target_pairs={{0,16},{16,0},{1,17},{17,1},{2,18},{18,2},{3,19},{19,3},{4,20},{20... | collective-permute-start | bytes 983048 | tf_op jit(solution)/shard_map/ppermute | solution.py:767
  289.6 2.8 margin_terms.3
  292.4 9.5 %collective-permute-start.44 = (f32[4,160,128]{2,1,0:T(8,128)}, f32[4,160,128]{2,1,0:T(8,128)S(1)}, u32[]{:S(2)}, u32[]{:S(2)}) collective-permute-start(f32[4,160,128]{2,1,0:T(8,128)} %get-tuple-element.116), channel_id=1, source_target_pairs={{0,16},{16,0},{1,17},{17,1},{2,18},{18,2},{3,19},{19,3},{4,20},{20... | collective-permute-start | bytes 983048 | tf_op jit(solution)/shard_map/ppermute | solution.py:767
  309.0 1.8 collective-permute-done.46.refs_2_
  310.8 2.0 collective-permute-done.47.refs_3_
  313.4 1.8 owner_rows.1
  320.5 2.8 collective-permute-done.49
  327.0 2.0 collective-permute-start.53
  329.0 5.1 %lay_out.1 = f32[128,4,16,128]{3,2,1,0:T(8,128)} custom-call(s32[5]{0:T(128)} %stack.70.state_ref, f32[128,2048]{1,0:T(8,128)} %round_piece.4.refs_0_, f32[128,2048]{1,0:T(8,128)} %round_piece.5.refs_1_, f32[128,2048]{1,0:T(8,128)} %round_piece.6.refs_2_, f32[128,2048]{1,0:T(8,128)} %round_piece.7.refs_3_, f32[128,2048]{1,0:T(8,128)} %get-tuple-element.108.refs_4_.refs_0_, ...), custom_call_target="tpu_custom_call" | custom-call | tf_op jit(solution)/shard_map/lay_out/pallas_call | solution.py:534
  336.3 2.0 pick.1
  (180 shorter events, 63.2 us)
Async XLA Ops:
  13.8 5.8 %collective-permute-start.1 = (f32[192,128]{1,0:T(8,128)S(1)}, f32[192,128]{1,0:T(8,128)S(1)}, u32[]{:S(2)}, u32[]{:S(2)}) collective-permute-start(f32[192,128]{1,0:T(8,128)S(1)} %broadcast_select_fusion.6), channel_id=1, source_target_pairs={{0,4},{4,0},{8,12},{12,8},{1,5},{5,1},{9,13},{13,9},{2,6},{6,2},{1... | collective-permute-start | bytes 294920 | tf_op jit(solution)/shard_map/ppermute | solution.py:767
  16.8 5.7 %collective-permute-start.2 = (f32[192,128]{1,0:T(8,128)S(1)}, f32[192,128]{1,0:T(8,128)S(1)}, u32[]{:S(2)}, u32[]{:S(2)}) collective-permute-start(f32[192,128]{1,0:T(8,128)S(1)} %broadcast_select_fusion.6), channel_id=1, source_target_pairs={{0,8},{4,12},{8,0},{12,4},{1,9},{5,13},{9,1},{13,5},{2,10},{6,14},... | collective-permute-start | bytes 294920 | tf_op jit(solution)/shard_map/ppermute | solution.py:767
  18.3 5.5 %collective-permute-start.3 = (f32[192,128]{1,0:T(8,128)S(1)}, f32[192,128]{1,0:T(8,128)S(1)}, u32[]{:S(2)}, u32[]{:S(2)}) collective-permute-start(f32[192,128]{1,0:T(8,128)S(1)} %broadcast_select_fusion.6), channel_id=1, source_target_pairs={{0,12},{4,8},{8,4},{12,0},{1,13},{5,9},{9,5},{13,1},{2,14},{6,10},... | collective-permute-start | bytes 294920 | tf_op jit(solution)/shard_map/ppermute | solution.py:767
  43.0 1.9 collective-permute-start.5
  44.9 5.5 %collective-permute-start.6 = (f32[192,128]{1,0:T(8,128)S(1)}, f32[192,128]{1,0:T(8,128)S(1)}, u32[]{:S(2)}, u32[]{:S(2)}) collective-permute-start(f32[192,128]{1,0:T(8,128)S(1)} %broadcast_select_fusion.8), channel_id=1, source_target_pairs={{0,4},{4,0},{8,12},{12,8},{1,5},{5,1},{9,13},{13,9},{2,6},{6,2},{1... | collective-permute-start | bytes 294920 | tf_op jit(solution)/shard_map/ppermute | solution.py:767
  45.5 7.8 %collective-permute-start.7 = (f32[192,128]{1,0:T(8,128)S(1)}, f32[192,128]{1,0:T(8,128)S(1)}, u32[]{:S(2)}, u32[]{:S(2)}) collective-permute-start(f32[192,128]{1,0:T(8,128)S(1)} %broadcast_select_fusion.8), channel_id=1, source_target_pairs={{0,8},{4,12},{8,0},{12,4},{1,9},{5,13},{9,1},{13,5},{2,10},{6,14},... | collective-permute-start | bytes 294920 | tf_op jit(solution)/shard_map/ppermute | solution.py:767
  46.0 7.3 %collective-permute-start.8 = (f32[192,128]{1,0:T(8,128)S(1)}, f32[192,128]{1,0:T(8,128)S(1)}, u32[]{:S(2)}, u32[]{:S(2)}) collective-permute-start(f32[192,128]{1,0:T(8,128)S(1)} %broadcast_select_fusion.8), channel_id=1, source_target_pairs={{0,12},{4,8},{8,4},{12,0},{1,13},{5,9},{9,5},{13,1},{2,14},{6,10},... | collective-permute-start | bytes 294920 | tf_op jit(solution)/shard_map/ppermute | solution.py:767
  48.5 30.6 %collective-permute-start.15 = (f32[256,128]{1,0:T(8,128)S(1)}, f32[256,128]{1,0:T(8,128)S(1)}, u32[]{:S(2)}, u32[]{:S(2)}) collective-permute-start(f32[256,128]{1,0:T(8,128)S(1)} %copy-done.12), channel_id=1, source_target_pairs={{0,16},{16,0},{1,17},{17,1},{2,18},{18,2},{3,19},{19,3},{4,20},{20... | collective-permute-start | bytes 393224 | tf_op jit(solution)/shard_map/ppermute | solution.py:767
  54.1 29.7 %collective-permute-start.17 = (f32[256,256]{1,0:T(8,128)}, f32[256,256]{1,0:T(8,128)S(1)}, u32[]{:S(2)}, u32[]{:S(2)}) collective-permute-start(f32[256,256]{1,0:T(8,128)} %get-tuple-element.89.inv_any), channel_id=1, source_target_pairs={{0,16},{16,0},{1,17},{17,1},{2,18},{18,2},{3,19},{19,3},{4,20},{20... | collective-permute-start | bytes 786440 | tf_op jit(solution)/shard_map/ppermute | solution.py:767
  61.7 18.5 %collective-permute-start.10 = (f32[192,128]{1,0:T(8,128)}, f32[192,128]{1,0:T(8,128)S(1)}, u32[]{:S(2)}, u32[]{:S(2)}) collective-permute-start(f32[192,128]{1,0:T(8,128)} %get-tuple-element.92), channel_id=1, source_target_pairs={{0,16},{16,0},{1,17},{17,1},{2,18},{18,2},{3,19},{19,3},{4,20},{20... | collective-permute-start | bytes 294920 | tf_op jit(solution)/shard_map/ppermute | solution.py:767
  79.8 10.1 %collective-permute-start.16 = (f32[256,256]{1,0:T(8,128)S(1)}, f32[256,256]{1,0:T(8,128)S(1)}, u32[]{:S(2)}, u32[]{:S(2)}) collective-permute-start(f32[256,256]{1,0:T(8,128)S(1)} %copy-done.7), channel_id=1, source_target_pairs={{0,16},{16,0},{1,17},{17,1},{2,18},{18,2},{3,19},{19,3},{4,20},{20... | collective-permute-start | bytes 786440 | tf_op jit(solution)/shard_map/ppermute | solution.py:767
  80.3 5.5 %collective-permute-start.11 = (f32[192,128]{1,0:T(8,128)S(1)}, f32[192,128]{1,0:T(8,128)S(1)}, u32[]{:S(2)}, u32[]{:S(2)}) collective-permute-start(f32[192,128]{1,0:T(8,128)S(1)} %broadcast_select_fusion.7), channel_id=1, source_target_pairs={{0,4},{4,0},{8,12},{12,8},{1,5},{5,1},{9,13},{13,9},{2,6},{6,2},{1... | collective-permute-start | bytes 294920 | tf_op jit(solution)/shard_map/ppermute | solution.py:767
  81.9 7.8 %collective-permute-start.12 = (f32[192,128]{1,0:T(8,128)S(1)}, f32[192,128]{1,0:T(8,128)S(1)}, u32[]{:S(2)}, u32[]{:S(2)}) collective-permute-start(f32[192,128]{1,0:T(8,128)S(1)} %broadcast_select_fusion.7), channel_id=1, source_target_pairs={{0,8},{4,12},{8,0},{12,4},{1,9},{5,13},{9,1},{13,5},{2,10},{6,14},... | collective-permute-start | bytes 294920 | tf_op jit(solution)/shard_map/ppermute | solution.py:767
  82.4 7.3 %collective-permute-start.13 = (f32[192,128]{1,0:T(8,128)S(1)}, f32[192,128]{1,0:T(8,128)S(1)}, u32[]{:S(2)}, u32[]{:S(2)}) collective-permute-start(f32[192,128]{1,0:T(8,128)S(1)} %broadcast_select_fusion.7), channel_id=1, source_target_pairs={{0,12},{4,8},{8,4},{12,0},{1,13},{5,9},{9,5},{13,1},{2,14},{6,10},... | collective-permute-start | bytes 294920 | tf_op jit(solution)/shard_map/ppermute | solution.py:767
  120.8 5.4 %collective-permute-start.19 = (f32[192,128]{1,0:T(8,128)S(1)}, f32[192,128]{1,0:T(8,128)S(1)}, u32[]{:S(2)}, u32[]{:S(2)}) collective-permute-start(f32[192,128]{1,0:T(8,128)S(1)} %broadcast_select_fusion.5), channel_id=1, source_target_pairs={{0,4},{4,0},{8,12},{12,8},{1,5},{5,1},{9,13},{13,9},{2,6},{6,2},{1... | collective-permute-start | bytes 294920 | tf_op jit(solution)/shard_map/ppermute | solution.py:767
  121.3 5.4 %collective-permute-start.20 = (f32[192,128]{1,0:T(8,128)S(1)}, f32[192,128]{1,0:T(8,128)S(1)}, u32[]{:S(2)}, u32[]{:S(2)}) collective-permute-start(f32[192,128]{1,0:T(8,128)S(1)} %broadcast_select_fusion.5), channel_id=1, source_target_pairs={{0,8},{4,12},{8,0},{12,4},{1,9},{5,13},{9,1},{13,5},{2,10},{6,14},... | collective-permute-start | bytes 294920 | tf_op jit(solution)/shard_map/ppermute | solution.py:767
  122.2 5.6 %collective-permute-start.21 = (f32[192,128]{1,0:T(8,128)S(1)}, f32[192,128]{1,0:T(8,128)S(1)}, u32[]{:S(2)}, u32[]{:S(2)}) collective-permute-start(f32[192,128]{1,0:T(8,128)S(1)} %broadcast_select_fusion.5), channel_id=1, source_target_pairs={{0,12},{4,8},{8,4},{12,0},{1,13},{5,9},{9,5},{13,1},{2,14},{6,10},... | collective-permute-start | bytes 294920 | tf_op jit(solution)/shard_map/ppermute | solution.py:767
  143.1 40.4 %collective-permute-start.24 = (f32[128,2048]{1,0:T(8,128)}, f32[128,2048]{1,0:T(8,128)S(1)}, u32[]{:S(2)}, u32[]{:S(2)}) collective-permute-start(f32[128,2048]{1,0:T(8,128)} %round_piece.6.refs_2_), channel_id=1, source_target_pairs={{0,2},{1,3},{2,0},{3,1},{4,6},{5,7},{6,4},{7,5},{8,10},{9,11},{10,... | collective-permute-start | bytes 3145736 | tf_op jit(solution)/shard_map/ppermute | solution.py:776
  151.6 49.9 %collective-permute-start.25 = (f32[128,2048]{1,0:T(8,128)}, f32[128,2048]{1,0:T(8,128)}, u32[]{:S(2)}, u32[]{:S(2)}) collective-permute-start(f32[128,2048]{1,0:T(8,128)} %round_piece.7.refs_3_), channel_id=1, source_target_pairs={{0,3},{1,2},{2,1},{3,0},{4,7},{5,6},{6,5},{7,4},{8,11},{9,10},{10,... | collective-permute-start | bytes 3145736 | tf_op jit(solution)/shard_map/ppermute | solution.py:776
  158.6 43.0 %collective-permute-start.23 = (f32[128,2048]{1,0:T(8,128)}, f32[128,2048]{1,0:T(8,128)}, u32[]{:S(2)}, u32[]{:S(2)}) collective-permute-start(f32[128,2048]{1,0:T(8,128)} %round_piece.5.refs_1_), channel_id=1, source_target_pairs={{0,1},{1,0},{2,3},{3,2},{4,5},{5,4},{6,7},{7,6},{8,9},{9,8},{10,11... | collective-permute-start | bytes 3145736 | tf_op jit(solution)/shard_map/ppermute | solution.py:776
  160.7 36.6 %collective-permute-start.26 = (f32[256,128]{1,0:T(8,128)S(1)}, f32[256,128]{1,0:T(8,128)S(1)}, u32[]{:S(2)}, u32[]{:S(2)}) collective-permute-start(f32[256,128]{1,0:T(8,128)S(1)} %copy-done), channel_id=1, source_target_pairs={{0,1},{1,0},{2,3},{3,2},{4,5},{5,4},{6,7},{7,6},{8,9},{9,8},{10,11... | collective-permute-start | bytes 393224 | tf_op jit(solution)/shard_map/ppermute | solution.py:776
  164.4 37.1 %collective-permute-start.27 = (f32[256,128]{1,0:T(8,128)S(1)}, f32[256,128]{1,0:T(8,128)S(1)}, u32[]{:S(2)}, u32[]{:S(2)}) collective-permute-start(f32[256,128]{1,0:T(8,128)S(1)} %copy-done), channel_id=1, source_target_pairs={{0,2},{1,3},{2,0},{3,1},{4,6},{5,7},{6,4},{7,5},{8,10},{9,11},{10,... | collective-permute-start | bytes 393224 | tf_op jit(solution)/shard_map/ppermute | solution.py:776
  183.4 18.1 %collective-permute-start.28 = (f32[256,128]{1,0:T(8,128)S(1)}, f32[256,128]{1,0:T(8,128)}, u32[]{:S(2)}, u32[]{:S(2)}) collective-permute-start(f32[256,128]{1,0:T(8,128)S(1)} %copy-done), channel_id=1, source_target_pairs={{0,3},{1,2},{2,1},{3,0},{4,7},{5,6},{6,5},{7,4},{8,11},{9,10},{10,... | collective-permute-start | bytes 393224 | tf_op jit(solution)/shard_map/ppermute | solution.py:776
  197.4 4.2 %collective-permute-start.29 = (f32[8,128]{1,0:T(8,128)S(1)}, f32[8,128]{1,0:T(8,128)S(1)}, u32[]{:S(2)}, u32[]{:S(2)}) collective-permute-start(f32[8,128]{1,0:T(8,128)S(1)} %slice.89), channel_id=1, source_target_pairs={{0,16},{16,0},{1,17},{17,1},{2,18},{18,2},{3,19},{19,3},{4,20},{20... | collective-permute-start | bytes 12296 | tf_op jit(solution)/shard_map/ppermute | solution.py:767
  215.8 1.9 collective-permute-start.30
  218.7 6.8 %collective-permute-start.31 = (f32[160,128]{1,0:T(8,128)S(1)}, f32[160,128]{1,0:T(8,128)S(1)}, u32[]{:S(2)}, u32[]{:S(2)}) collective-permute-start(f32[160,128]{1,0:T(8,128)S(1)} %get-tuple-element.123), channel_id=1, source_target_pairs={{0,4},{4,0},{8,12},{12,8},{1,5},{5,1},{9,13},{13,9},{2,6},{6,2},{1... | collective-permute-start | bytes 245768 | tf_op jit(solution)/shard_map/ppermute | solution.py:767
  220.2 7.0 %collective-permute-start.32 = (f32[160,128]{1,0:T(8,128)S(1)}, f32[160,128]{1,0:T(8,128)S(1)}, u32[]{:S(2)}, u32[]{:S(2)}) collective-permute-start(f32[160,128]{1,0:T(8,128)S(1)} %get-tuple-element.122), channel_id=1, source_target_pairs={{0,8},{4,12},{8,0},{12,4},{1,9},{5,13},{9,1},{13,5},{2,10},{6,14},... | collective-permute-start | bytes 245768 | tf_op jit(solution)/shard_map/ppermute | solution.py:767
  221.4 5.8 %collective-permute-start.33 = (f32[160,128]{1,0:T(8,128)S(1)}, f32[160,128]{1,0:T(8,128)S(1)}, u32[]{:S(2)}, u32[]{:S(2)}) collective-permute-start(f32[160,128]{1,0:T(8,128)S(1)} %get-tuple-element.121), channel_id=1, source_target_pairs={{0,12},{4,8},{8,4},{12,0},{1,13},{5,9},{9,5},{13,1},{2,14},{6,10},... | collective-permute-start | bytes 245768 | tf_op jit(solution)/shard_map/ppermute | solution.py:767
  222.3 66.0 %collective-permute-start.41 = (f32[128,2048]{1,0:T(8,128)S(1)}, f32[128,2048]{1,0:T(8,128)}, u32[]{:S(2)}, u32[]{:S(2)}) collective-permute-start(f32[128,2048]{1,0:T(8,128)S(1)} %copy-done.5), channel_id=1, source_target_pairs={{16,17},{17,16},{18,19},{19,18},{20,21},{21,20},{22,23},{23,22},{2... | collective-permute-start | bytes 3145736 | tf_op jit(solution)/shard_map/ppermute | solution.py:776
  223.9 64.4 %collective-permute-start.42 = (f32[128,2048]{1,0:T(8,128)S(1)}, f32[128,2048]{1,0:T(8,128)}, u32[]{:S(2)}, u32[]{:S(2)}) collective-permute-start(f32[128,2048]{1,0:T(8,128)S(1)} %copy-done.6), channel_id=1, source_target_pairs={{16,18},{17,19},{18,16},{19,17},{20,22},{21,23},{22,20},{23,21},{2... | collective-permute-start | bytes 3145736 | tf_op jit(solution)/shard_map/ppermute | solution.py:776
  225.5 62.8 %collective-permute-start.43 = (f32[128,2048]{1,0:T(8,128)}, f32[128,2048]{1,0:T(8,128)}, u32[]{:S(2)}, u32[]{:S(2)}) collective-permute-start(f32[128,2048]{1,0:T(8,128)} %get-tuple-element.111.refs_7_), channel_id=1, source_target_pairs={{16,19},{17,18},{18,17},{19,16},{20,23},{21,22},{22,21},{23,20},{2... | collective-permute-start | bytes 3145736 | tf_op jit(solution)/shard_map/ppermute | solution.py:776
  227.2 13.6 %collective-permute-start.34 = (f32[160,128]{1,0:T(8,128)S(1)}, f32[160,128]{1,0:T(8,128)S(1)}, u32[]{:S(2)}, u32[]{:S(2)}) collective-permute-start(f32[160,128]{1,0:T(8,128)S(1)} %fusion.1), channel_id=1, source_target_pairs={{0,1},{1,0},{2,3},{3,2},{4,5},{5,4},{6,7},{7,6},{8,9},{9,8},{10,11... | collective-permute-start | bytes 245768 | tf_op jit(solution)/shard_map/ppermute | solution.py:767
  227.3 13.9 %collective-permute-start.35 = (f32[160,128]{1,0:T(8,128)S(1)}, f32[160,128]{1,0:T(8,128)S(1)}, u32[]{:S(2)}, u32[]{:S(2)}) collective-permute-start(f32[160,128]{1,0:T(8,128)S(1)} %fusion.1), channel_id=1, source_target_pairs={{0,2},{1,3},{2,0},{3,1},{4,6},{5,7},{6,4},{7,5},{8,10},{9,11},{10,... | collective-permute-start | bytes 245768 | tf_op jit(solution)/shard_map/ppermute | solution.py:767
  240.8 7.2 %collective-permute-start.36 = (f32[160,128]{1,0:T(8,128)S(1)}, f32[160,128]{1,0:T(8,128)S(1)}, u32[]{:S(2)}, u32[]{:S(2)}) collective-permute-start(f32[160,128]{1,0:T(8,128)S(1)} %fusion.1), channel_id=1, source_target_pairs={{0,3},{1,2},{2,1},{3,0},{4,7},{5,6},{6,5},{7,4},{8,11},{9,10},{10,... | collective-permute-start | bytes 245768 | tf_op jit(solution)/shard_map/ppermute | solution.py:767
  248.0 4.5 %collective-permute-start.37 = (f32[160,128]{1,0:T(8,128)S(1)}, f32[160,128]{1,0:T(8,128)S(1)}, u32[]{:S(2)}, u32[]{:S(2)}) collective-permute-start(f32[160,128]{1,0:T(8,128)S(1)} %add_add_fusion.4), channel_id=1, source_target_pairs={{0,4},{4,0},{8,12},{12,8},{1,5},{5,1},{9,13},{13,9},{2,6},{6,2},{1... | collective-permute-start | bytes 245768 | tf_op jit(solution)/shard_map/ppermute | solution.py:767
  249.6 5.0 %collective-permute-start.38 = (f32[160,128]{1,0:T(8,128)S(1)}, f32[160,128]{1,0:T(8,128)S(1)}, u32[]{:S(2)}, u32[]{:S(2)}) collective-permute-start(f32[160,128]{1,0:T(8,128)S(1)} %add_add_fusion.4), channel_id=1, source_target_pairs={{0,8},{4,12},{8,0},{12,4},{1,9},{5,13},{9,1},{13,5},{2,10},{6,14},... | collective-permute-start | bytes 245768 | tf_op jit(solution)/shard_map/ppermute | solution.py:767
  252.5 5.3 %collective-permute-start.39 = (f32[160,128]{1,0:T(8,128)S(1)}, f32[160,128]{1,0:T(8,128)S(1)}, u32[]{:S(2)}, u32[]{:S(2)}) collective-permute-start(f32[160,128]{1,0:T(8,128)S(1)} %add_add_fusion.4), channel_id=1, source_target_pairs={{0,12},{4,8},{8,4},{12,0},{1,13},{5,9},{9,5},{13,1},{2,14},{6,10},... | collective-permute-start | bytes 245768 | tf_op jit(solution)/shard_map/ppermute | solution.py:767
  257.9 31.0 %collective-permute-start.40 = (f32[4,160,128]{2,1,0:T(8,128)S(1)}, f32[4,160,128]{2,1,0:T(8,128)S(1)}, u32[]{:S(2)}, u32[]{:S(2)}) collective-permute-start(f32[4,160,128]{2,1,0:T(8,128)S(1)} %pad_maximum_fusion.refs_8_.own_ref), channel_id=1, source_target_pairs={{0,16},{16,0},{1,17},{17,1},{2,18},{18,2},{3,19},{19,3},{4,20},{20... | collective-permute-start | bytes 983048 | tf_op jit(solution)/shard_map/ppermute | solution.py:767
  292.4 11.0 %collective-permute-start.44 = (f32[4,160,128]{2,1,0:T(8,128)}, f32[4,160,128]{2,1,0:T(8,128)S(1)}, u32[]{:S(2)}, u32[]{:S(2)}) collective-permute-start(f32[4,160,128]{2,1,0:T(8,128)} %get-tuple-element.116), channel_id=1, source_target_pairs={{0,16},{16,0},{1,17},{17,1},{2,18},{18,2},{3,19},{19,3},{4,20},{20... | collective-permute-start | bytes 983048 | tf_op jit(solution)/shard_map/ppermute | solution.py:767
  304.1 4.9 %collective-permute-start.45 = (f32[160,128]{1,0:T(8,128)S(1)}, f32[160,128]{1,0:T(8,128)S(1)}, u32[]{:S(2)}, u32[]{:S(2)}) collective-permute-start(f32[160,128]{1,0:T(8,128)S(1)} %get-tuple-element.119), channel_id=1, source_target_pairs={{0,4},{4,0},{8,12},{12,8},{1,5},{5,1},{9,13},{13,9},{2,6},{6,2},{1... | collective-permute-start | bytes 245768 | tf_op jit(solution)/shard_map/ppermute | solution.py:767
  305.6 5.2 %collective-permute-start.46 = (f32[160,128]{1,0:T(8,128)S(1)}, f32[160,128]{1,0:T(8,128)S(1)}, u32[]{:S(2)}, u32[]{:S(2)}) collective-permute-start(f32[160,128]{1,0:T(8,128)S(1)} %get-tuple-element.118), channel_id=1, source_target_pairs={{0,8},{4,12},{8,0},{12,4},{1,9},{5,13},{9,1},{13,5},{2,10},{6,14},... | collective-permute-start | bytes 245768 | tf_op jit(solution)/shard_map/ppermute | solution.py:767
  306.7 6.0 %collective-permute-start.47 = (f32[160,128]{1,0:T(8,128)S(1)}, f32[160,128]{1,0:T(8,128)S(1)}, u32[]{:S(2)}, u32[]{:S(2)}) collective-permute-start(f32[160,128]{1,0:T(8,128)S(1)} %get-tuple-element.117), channel_id=1, source_target_pairs={{0,12},{4,8},{8,4},{12,0},{1,13},{5,9},{9,5},{13,1},{2,14},{6,10},... | collective-permute-start | bytes 245768 | tf_op jit(solution)/shard_map/ppermute | solution.py:767
  316.0 4.4 %collective-permute-start.48 = (f32[64,128]{1,0:T(8,128)S(1)}, f32[64,128]{1,0:T(8,128)S(1)}, u32[]{:S(2)}, u32[]{:S(2)}) collective-permute-start(f32[64,128]{1,0:T(8,128)S(1)} %get-tuple-element.126), channel_id=1, source_target_pairs={{0,1},{1,0},{2,3},{3,2},{4,5},{5,4},{6,7},{7,6},{8,9},{9,8},{10,11... | collective-permute-start | bytes 98312 | tf_op jit(solution)/shard_map/ppermute | solution.py:767
  317.5 5.7 %collective-permute-start.49 = (f32[64,128]{1,0:T(8,128)S(1)}, f32[64,128]{1,0:T(8,128)S(1)}, u32[]{:S(2)}, u32[]{:S(2)}) collective-permute-start(f32[64,128]{1,0:T(8,128)S(1)} %get-tuple-element.125), channel_id=1, source_target_pairs={{0,2},{1,3},{2,0},{3,1},{4,6},{5,7},{6,4},{7,5},{8,10},{9,11},{10,... | collective-permute-start | bytes 98312 | tf_op jit(solution)/shard_map/ppermute | solution.py:767
  319.0 5.7 %collective-permute-start.50 = (f32[64,128]{1,0:T(8,128)S(1)}, f32[64,128]{1,0:T(8,128)S(1)}, u32[]{:S(2)}, u32[]{:S(2)}) collective-permute-start(f32[64,128]{1,0:T(8,128)S(1)} %get-tuple-element.124), channel_id=1, source_target_pairs={{0,3},{1,2},{2,1},{3,0},{4,7},{5,6},{6,5},{7,4},{8,11},{9,10},{10,... | collective-permute-start | bytes 98312 | tf_op jit(solution)/shard_map/ppermute | solution.py:767
  325.5 8.7 %collective-permute-start.51 = (f32[64,128]{1,0:T(8,128)S(1)}, f32[64,128]{1,0:T(8,128)S(1)}, u32[]{:S(2)}, u32[]{:S(2)}) collective-permute-start(f32[64,128]{1,0:T(8,128)S(1)} %fusion.3), channel_id=1, source_target_pairs={{0,4},{4,0},{8,12},{12,8},{1,5},{5,1},{9,13},{13,9},{2,6},{6,2},{1... | collective-permute-start | bytes 98312 | tf_op jit(solution)/shard_map/ppermute | solution.py:767
  326.1 8.1 %collective-permute-start.52 = (f32[64,128]{1,0:T(8,128)S(1)}, f32[64,128]{1,0:T(8,128)S(1)}, u32[]{:S(2)}, u32[]{:S(2)}) collective-permute-start(f32[64,128]{1,0:T(8,128)S(1)} %fusion.3), channel_id=1, source_target_pairs={{0,8},{4,12},{8,0},{12,4},{1,9},{5,13},{9,1},{13,5},{2,10},{6,14},... | collective-permute-start | bytes 98312 | tf_op jit(solution)/shard_map/ppermute | solution.py:767
  327.0 7.1 %collective-permute-start.53 = (f32[64,128]{1,0:T(8,128)S(1)}, f32[64,128]{1,0:T(8,128)S(1)}, u32[]{:S(2)}, u32[]{:S(2)}) collective-permute-start(f32[64,128]{1,0:T(8,128)S(1)} %fusion.3), channel_id=1, source_target_pairs={{0,12},{4,8},{8,4},{12,0},{1,13},{5,9},{9,5},{13,1},{2,14},{6,10},... | collective-permute-start | bytes 98312 | tf_op jit(solution)/shard_map/ppermute | solution.py:767
  (40 other events, 272.7 us)

commit v2 on v1

--- a/solution.py
+++ b/solution.py
@@ -30,6 +30,10 @@
 def split(value):
     high = value.astype(BF16)
     return high, (value - high.astype(F32)).astype(BF16)
+
+
+def room(mebibytes):
+    return pltpu.CompilerParams(vmem_limit_bytes=mebibytes << 20)
 
 
 def tree_sum(terms):
@@ -170,6 +174,7 @@
         ),
         out_shape=[shape(dims) for dims in half_dims(width)],
         name="gram",
+        compiler_params=room(24),
     )(state, core)
 
 
@@ -278,6 +283,7 @@
         ),
         out_shape=[shape(dims) for dims in half_dims(width)] + [shape((rank, rank))] * 2,
         name="absorbed_gram",
+        compiler_params=room(20),
     )(state, *outer, core)
 
 
@@ -369,6 +375,7 @@
     scratch = [pltpu.VMEM((width, 2 * kept), BF16), pltpu.VMEM((rank, 2 * rank), F32)]
     operands = [core, right_map]
     if pieces:
+        out_shape[:2] = [pltpu.HBM((rank, mode_count * kept), BF16)] * 2
         away = pl.BlockSpec(
             (rank, modes * kept), lambda s, state: (0, state[1] ^ (s * (1 - state[0])))
         )
@@ -391,6 +398,7 @@
         ),
         out_shape=out_shape,
         name="project",
+        compiler_params=room(30),
     )(state, *operands)
 
 
@@ -464,6 +472,7 @@
             pltpu.SemaphoreType.DMA((2,)),
         ],
         name="basis",
+        compiler_params=room(8),
     )(state, *halves, sketch, lower, inverse)
 
 
@@ -491,6 +500,7 @@
         ),
         out_shape=shape((kept, width)),
         name="round_piece",
+        compiler_params=room(12),
     )(state, front, high, low)
 
 
@@ -543,6 +553,7 @@
             pltpu.SemaphoreType.DMA((pieces,)),
         ],
         name="lay_out",
+        compiler_params=room(16),
     )(state, *first, *last)
 
 
@@ -614,8 +625,8 @@
             for i, (p, q) in enumerate(pairs):
                 env = env_in_ref[i * kept : (i + 1) * kept]
                 env_high, env_low = split(env)
-                env_ref[q, p * kept : (p + 1) * kept] = env_high
-                env_ref[q, (count + p) * kept : (count + p + 1) * kept] = env_low
+                env_ref[q, p * kept : (p + 1) * kept, :kept] = env_high
+                env_ref[q, p * kept : (p + 1) * kept, kept:] = env_low
 
         for d in range(count):
             stage_ref[me ^ d] = piece_refs[d][...]
@@ -632,10 +643,10 @@
             highs.append(tall(high))
             lows.append(tall(low))
             rows = (q + 1) * kept
-            env_high = env_ref[q, :rows]
-            env_low = env_ref[q, count * kept : count * kept + rows]
-            stacked = contract(jnp.concatenate([env_high, env_low], axis=0), high, 1, 0)
-            moved = stacked[:rows] + (stacked[rows:] + contract(env_high, low, 1, 0))
+            env = env_ref[q, :rows]
+            moved = contract(env, jnp.concatenate([high, high], axis=0), 1, 0) + contract(
+                env, jnp.concatenate([low, low], axis=0), 1, 0
+            )
             for p in range(q + 1):
                 carried[p, q] = split(tall(moved[p * kept : (p + 1) * kept]))
         for p in range(count):
@@ -675,7 +686,7 @@
     part = env[0].shape
     scratch = [
         pltpu.VMEM((count, kept, chunk), F32),
-        pltpu.VMEM((count, 2 * count * kept, kept), BF16),
+        pltpu.VMEM((count, count * kept, 2 * kept), BF16),
         pltpu.VMEM((total, kept), F32),
         pltpu.VMEM((count, *frames[0].shape), F32),
         pltpu.VMEM(part, F32),
@@ -694,12 +705,13 @@
         ),
         out_shape=[shape(part)] * 2,
         name="margin_terms",
+        compiler_params=room(20),
     )(state, *pieces, *frames, *env, token)
 
 
 def unset(dims):
     return pl.pallas_call(
-        lambda ref: None, out_specs=ANY, out_shape=shape(dims), name="unset"
+        lambda ref: None, out_specs=ANY, out_shape=shape(dims), name="unset", compiler_params=room(2)
     )()
 
 
@@ -729,6 +741,7 @@
         out_shape=shape((count, count * size, kept)),
         scratch_shapes=[pltpu.VMEM((rows, kept), F32)],
         name="owner_rows",
+        compiler_params=room(4),
     )(state, *parts)
 
 
@@ -760,6 +773,7 @@
         out_shape=shape((kept, count * kept)),
         scratch_shapes=[pltpu.VMEM((count * (count + 1) // 2 * kept, kept), F32)],
         name="pick",
+        compiler_params=room(6),
     )(state, *env_first, *env_last)
 
 
@@ -781,7 +795,7 @@
 
 
 def local(train_cores, sketch, exit_sketch):
-    core = train_cores[0]
+    core = pltpu.with_memory_space_constraint(train_cores[0], pltpu.HBM)
     rank, mode_count, _ = core.shape
     kept = sketch.shape[1]
     row_size = lax.axis_size("row")
@@ -851,11 +865,12 @@
         own_last = [
             round_piece(at(state_last, d), *rounded_last, vec_size) for d in range(vec_size)
         ]
-    left_first = row_total(*left_first, 0)
-    *own_last, left_own, left_other = lax.optimization_barrier((*own_last, *left_first))
-    left_first = (left_own, left_other)
+    first_high, first_low = (
+        pltpu.with_memory_space_constraint(x, pltpu.HBM) for x in (first_high, first_low)
+    )
     pieces_last = list(own_last)
     sent(pieces_last, 1, [d for d in range(1, vec_size) if d not in late])
+    left_first = row_total(*left_first, 0)
     frame_first, _, _ = basis(state_first, left_first, sketch, lower, inverse)
     own_first = [None] * vec_size
     for d in range(vec_size - 1, -1, -1):

time: 339 us -> 309 us (0.912)
  Pallas kernels: 109 us -> 90.7 us
  local copies, waits for them, and re-layouts: 10.9 us -> 2.4 us
  other arithmetic: 6.66 us -> 1.79 us
  waiting for transfers between devices: 84.8 us -> 89.4 us
    unnamed x70 -> x28, local copies, waits for them, and re-layouts: 6.81 us -> 1.94 us
    pallas_call x2, Pallas kernels: 15.8 us -> 11.5 us  [margin_terms(): pl.pallas_call(functools.partial(margin_body, count), grid_spec=pltpu.Pre...]
    ppermute x46, waiting for transfers between devices: 60.8 us -> 64.4 us  [send(): return lax.ppermute(block, axis, [(i, i ^ distance) for i in range(size)])]
  transfers between devices with their start and end apart: 55 -> 55, of which waited for: 33 -> 34; matrix products, arithmetic and copies ran while one was open for 1% -> 1% of each run, Pallas kernels for 7% -> 5%
where the time goes in v2:
time: 309 us; the launch traced here: 308 us
  starting transfers between devices  123 us (40%)
  Pallas kernels  90.7 us (29%)
  waiting for transfers between devices  89.4 us (29%)
    ppermute x46, starting transfers between devices, send(): return lax.ppermute(block, axis, [(i, i ^ distance) for i in range(size)])  95.3 us
    ppermute x46, waiting for transfers between devices, send(): return lax.ppermute(block, axis, [(i, i ^ distance) for i in range(size)])  64.4 us
    ppermute x9, starting transfers between devices, send_from(): return lax.ppermute(block, ('cores', 'vec'), pairs)  27.5 us
    ppermute x9, waiting for transfers between devices, send_from(): return lax.ppermute(block, ('cores', 'vec'), pairs)  24.9 us
    pallas_call x3, Pallas kernels, basis(): pl.pallas_call(basis_body, in_specs=[SMEM] + [VMEM] * 3 + [ANY] * 2, out_...  20.5 us
    pallas_call x2, Pallas kernels, project(): pl.pallas_call(functools.partial(project_body, pieces, len(half_shapes)),...  16.7 us
    pallas_call x1, Pallas kernels, absorbed_gram(): pl.pallas_call(absorbed_body, grid_spec=pltpu.PrefetchScalarGridSpec(num_...  16.1 us
    pallas_call x2, Pallas kernels, margin_terms(): pl.pallas_call(functools.partial(margin_body, count), grid_spec=pltpu.Pre...  11.5 us
  transfers between devices with their start and end apart: 55, of which 34 were waited for; matrix products, arithmetic and copies ran while one was open for 1% of the time, Pallas kernels for 5%

profile of v2, /device:TPU:0, one launch (start us, length us, event | category | flops | bytes accessed | tf_op | source)
XLA Modules:
  0.0 308.3 jit_solution(1039764602956554466)
XLA Ops:
  0.7 9.3 %gram.1 = (f32[192,128]{1,0:T(8,128)S(1)}, f32[192,128]{1,0:T(8,128)S(1)}) custom-call(s32[5]{0:T(128)S(1)} %stack.72.state_ref, f32[256,64,256]{2,1,0:T(8,128)} %bitcast.53), custom_call_target="tpu_custom_call" | custom-call | tf_op jit(solution)/shard_map/gram/pallas_call | solution.py:166
  11.4 3.0 collective-permute-start.1
  16.0 1.6 collective-permute-done.1
  17.6 2.6 collective-permute-done.2
  22.9 16.1 %absorbed_gram.1 = (f32[192,128]{1,0:T(8,128)S(1)}, f32[192,128]{1,0:T(8,128)S(1)}, f32[256,256]{1,0:T(8,128)S(1)}, f32[256,256]{1,0:T(8,128)S(1)}) custom-call(s32[5]{0:T(128)S(1)} %stack.74.state_ref, f32[192,128]{1,0:T(8,128)S(1)} %add_add_fusion.3.own_ref, f32[192,128]{1,0:T(8,128)S(1)} %collective-permute-done.4.other_ref, f32[256,64,256]{2,1,0:T(8,128)} %bitcast.54), custom_call_target="tpu_custom_call" | custom-call | tf_op jit(solution)/shard_map/absorbed_gram/pallas_call | solution.py:270
  42.4 1.8 collective-permute-start.8
  44.2 1.9 collective-permute-done.6
  51.4 3.0 project.2
  54.3 16.7 %collective-permute-start.10 = (f32[192,128]{1,0:T(8,128)S(1)}, f32[192,128]{1,0:T(8,128)S(1)}, u32[]{:S(2)}, u32[]{:S(2)}) collective-permute-start(f32[192,128]{1,0:T(8,128)S(1)} %get-tuple-element.86), channel_id=1, source_target_pairs={{0,16},{16,0},{1,17},{17,1},{2,18},{18,2},{3,19},{19,3},{4,20},{20... | collective-permute-start | bytes 294920 | tf_op jit(solution)/shard_map/ppermute | solution.py:781
  75.6 1.6 collective-permute-done.11
  77.2 2.8 collective-permute-done.12
  81.4 9.9 %basis.4 = (f32[256,128]{1,0:T(8,128)S(1)}, f32[256,128]{1,0:T(8,128)S(1)}, f32[256,128]{1,0:T(8,128)S(1)}) custom-call(s32[5]{0:T(128)S(1)} %stack.70.state_ref, f32[192,128]{1,0:T(8,128)S(1)} %add_add_fusion.1.own_ref, f32[192,128]{1,0:T(8,128)S(1)} %collective-permute-done.14.other_ref, f32[256,128]{1,0:T(8,128)S(1)} %broadcast_select_fusion.4.sketch_ref, ...), custom_call_target="tpu_custom_call" | custom-call | tf_op jit(solution)/shard_map/basis/pallas_call | solution.py:463
  91.4 13.8 %project.3 = (bf16[256,8192]{1,0:T(8,128)(2,1)}, bf16[256,8192]{1,0:T(8,128)(2,1)}, f32[192,128]{1,0:T(8,128)S(1)}, f32[192,128]{1,0:T(8,128)S(1)}, f32[128,2048...) custom-call(s32[5]{0:T(128)S(1)} %stack.72.state_ref, ...), custom_call_target="tpu_custom_call" | custom-call | tf_op jit(solution)/shard_map/project/pallas_call | solution.py:390
  108.3 1.8 collective-permute-start.21
  110.1 1.6 collective-permute-done.19
  115.7 9.2 %basis.5 = (f32[256,128]{1,0:T(8,128)S(1)}, f32[256,128]{1,0:T(8,128)}, f32[256,128]{1,0:T(8,128)}) custom-call(s32[5]{0:T(128)S(1)} %stack.72.state_ref, f32[192,128]{1,0:T(8,128)S(1)} %add_add_fusion.own_ref, f32[192,128]{1,0:T(8,128)S(1)} %collective-permute-done.22.other_ref, f32[256,128]{1,0:T(8,128)S(1)} %copy-done.8, ...), custom_call_target="tpu_custom_call" | custom-call | tf_op jit(solution)/shard_map/basis/pallas_call | solution.py:463
  124.8 2.7 round_piece.6.refs_2_
  127.6 4.5 %collective-permute-start.24 = (f32[128,2048]{1,0:T(8,128)S(1)}, f32[128,2048]{1,0:T(8,128)S(1)}, u32[]{:S(2)}, u32[]{:S(2)}) collective-permute-start(f32[128,2048]{1,0:T(8,128)S(1)} %round_piece.6.refs_2_), channel_id=1, source_target_pairs={{0,2},{1,3},{2,0},{3,1},{4,6},{5,7},{6,4},{7,5},{8,10},{9,11},{10,... | collective-permute-start | bytes 3145736 | tf_op jit(solution)/shard_map/ppermute | solution.py:790
  132.1 2.7 round_piece.7.refs_3_
  134.9 3.3 %collective-permute-start.25 = (f32[128,2048]{1,0:T(8,128)S(1)}, f32[128,2048]{1,0:T(8,128)S(1)}, u32[]{:S(2)}, u32[]{:S(2)}) collective-permute-start(f32[128,2048]{1,0:T(8,128)S(1)} %round_piece.7.refs_3_), channel_id=1, source_target_pairs={{0,3},{1,2},{2,1},{3,0},{4,7},{5,6},{6,5},{7,4},{8,11},{9,10},{10,... | collective-permute-start | bytes 3145736 | tf_op jit(solution)/shard_map/ppermute | solution.py:790
  138.1 2.7 round_piece.5.refs_1_
  140.9 2.1 collective-permute-start.23
  143.0 3.7 %collective-permute-start.26 = (f32[256,128]{1,0:T(8,128)S(1)}, f32[256,128]{1,0:T(8,128)S(1)}, u32[]{:S(2)}, u32[]{:S(2)}) collective-permute-start(f32[256,128]{1,0:T(8,128)S(1)} %get-tuple-element.93.front_ref.refs_4_), channel_id=1, source_target_pairs={{0,1},{1,0},{2,3},{3,2},{4,5},{5,4},{6,7},{7,6},{8,9},{9,8},{10,11... | collective-permute-start | bytes 393224 | tf_op jit(solution)/shard_map/ppermute | solution.py:790
  146.7 3.6 %collective-permute-start.27 = (f32[256,128]{1,0:T(8,128)S(1)}, f32[256,128]{1,0:T(8,128)S(1)}, u32[]{:S(2)}, u32[]{:S(2)}) collective-permute-start(f32[256,128]{1,0:T(8,128)S(1)} %get-tuple-element.93.front_ref.refs_4_), channel_id=1, source_target_pairs={{0,2},{1,3},{2,0},{3,1},{4,6},{5,7},{6,4},{7,5},{8,10},{9,11},{10,... | collective-permute-start | bytes 393224 | tf_op jit(solution)/shard_map/ppermute | solution.py:790
  150.3 17.4 %collective-permute-done.24.refs_2_ = f32[128,2048]{1,0:T(8,128)S(1)} collective-permute-done((f32[128,2048]{1,0:T(8,128)S(1)}, f32[128,2048]{1,0:T(8,128)S(1)}, u32[]{:S(2)}, u32[]{:S(2)}) %collective-permute-start.24) | collective-permute-done | bytes 1048608 | tf_op jit(solution)/shard_map/ppermute | solution.py:790
  167.7 5.4 %collective-permute-start.28 = (f32[256,128]{1,0:T(8,128)S(1)}, f32[256,128]{1,0:T(8,128)S(1)}, u32[]{:S(2)}, u32[]{:S(2)}) collective-permute-start(f32[256,128]{1,0:T(8,128)S(1)} %get-tuple-element.93.front_ref.refs_4_), channel_id=1, source_target_pairs={{0,3},{1,2},{2,1},{3,0},{4,7},{5,6},{6,5},{7,4},{8,11},{9,10},{10,... | collective-permute-start | bytes 393224 | tf_op jit(solution)/shard_map/ppermute | solution.py:790
  174.1 7.5 %collective-permute-done.26.refs_5_ = f32[256,128]{1,0:T(8,128)S(1)} collective-permute-done((f32[256,128]{1,0:T(8,128)S(1)}, f32[256,128]{1,0:T(8,128)S(1)}, u32[]{:S(2)}, u32[]{:S(2)}) %collective-permute-start.26) | collective-permute-done | bytes 131104 | tf_op jit(solution)/shard_map/ppermute | solution.py:790
  181.7 2.7 round_piece.4.refs_0_
  184.5 9.7 %margin_terms.2 = (f32[4,160,128]{2,1,0:T(8,128)S(1)}, f32[4,160,128]{2,1,0:T(8,128)S(1)}) custom-call(s32[5]{0:T(128)S(1)} %stack.72.state_ref, f32[128,2048]{1,0:T(8,128)S(1)} %round_piece.4.refs_0_, f32[128,2048]{1,0:T(8,128)S(1)} %collective-permute-done.23.refs_1_, f32[128,2048]{1,0:T(8,128)S(1)} %copy-done.5, ...), custom_call_target="tpu_custom_call" | custom-call | tf_op jit(solution)/shard_map/margin_terms/pallas_call | solution.py:697
  199.6 1.7 collective-permute-start.41
  201.3 1.6 collective-permute-start.42
  202.9 1.6 collective-permute-start.43
  205.3 3.3 %collective-permute-start.35 = (f32[160,128]{1,0:T(8,128)S(1)}, f32[160,128]{1,0:T(8,128)S(1)}, u32[]{:S(2)}, u32[]{:S(2)}) collective-permute-start(f32[160,128]{1,0:T(8,128)S(1)} %fusion.1), channel_id=1, source_target_pairs={{0,2},{1,3},{2,0},{3,1},{4,6},{5,7},{6,4},{7,5},{8,10},{9,11},{10,... | collective-permute-start | bytes 245768 | tf_op jit(solution)/shard_map/ppermute | solution.py:781
  208.7 11.0 %collective-permute-done.34 = f32[160,128]{1,0:T(8,128)S(1)} collective-permute-done((f32[160,128]{1,0:T(8,128)S(1)}, f32[160,128]{1,0:T(8,128)S(1)}, u32[]{:S(2)}, u32[]{:S(2)}) %collective-permute-start.34) | collective-permute-done | bytes 81952 | tf_op jit(solution)/shard_map/ppermute | solution.py:781
  220.1 6.7 %collective-permute-done.36 = f32[160,128]{1,0:T(8,128)S(1)} collective-permute-done((f32[160,128]{1,0:T(8,128)S(1)}, f32[160,128]{1,0:T(8,128)S(1)}, u32[]{:S(2)}, u32[]{:S(2)}) %collective-permute-start.36) | collective-permute-done | bytes 81952 | tf_op jit(solution)/shard_map/ppermute | solution.py:781
  229.2 2.2 collective-permute-done.37
  231.4 1.7 collective-permute-start.39
  233.1 3.6 %collective-permute-done.39 = f32[160,128]{1,0:T(8,128)S(1)} collective-permute-done((f32[160,128]{1,0:T(8,128)S(1)}, f32[160,128]{1,0:T(8,128)S(1)}, u32[]{:S(2)}, u32[]{:S(2)}) %collective-permute-start.39) | collective-permute-done | bytes 81952 | tf_op jit(solution)/shard_map/ppermute | solution.py:781
  237.5 29.3 %collective-permute-start.40 = (f32[4,160,128]{2,1,0:T(8,128)}, f32[4,160,128]{2,1,0:T(8,128)}, u32[]{:S(2)}, u32[]{:S(2)}) collective-permute-start(f32[4,160,128]{2,1,0:T(8,128)} %pad_maximum_fusion.refs_8_.own_ref), channel_id=1, source_target_pairs={{0,16},{16,0},{1,17},{17,1},{2,18},{18,2},{3,19},{19,3},{4,20},{20... | collective-permute-start | bytes 983048 | tf_op jit(solution)/shard_map/ppermute | solution.py:781
  269.3 1.7 margin_terms.3
  271.1 8.4 %collective-permute-start.44 = (f32[4,160,128]{2,1,0:T(8,128)S(1)}, f32[4,160,128]{2,1,0:T(8,128)S(1)}, u32[]{:S(2)}, u32[]{:S(2)}) collective-permute-start(f32[4,160,128]{2,1,0:T(8,128)S(1)} %get-tuple-element.104), channel_id=1, source_target_pairs={{0,16},{16,0},{1,17},{17,1},{2,18},{18,2},{3,19},{19,3},{4,20},{20... | collective-permute-start | bytes 983048 | tf_op jit(solution)/shard_map/ppermute | solution.py:781
  286.4 2.1 collective-permute-done.47.refs_3_
  290.7 1.8 collective-permute-start.49
  293.6 2.5 collective-permute-done.49
  296.1 2.1 collective-permute-done.50
  300.1 1.7 collective-permute-start.53
  301.8 3.1 %lay_out.1 = f32[128,4,16,128]{3,2,1,0:T(8,128)} custom-call(s32[5]{0:T(128)S(1)} %stack.70.state_ref, f32[128,2048]{1,0:T(8,128)S(1)} %round_piece.4.refs_0_, f32[128,2048]{1,0:T(8,128)S(1)} %copy-done.3, f32[128,2048]{1,0:T(8,128)S(1)} %round_piece.6.refs_2_, f32[128,2048]{1,0:T(8,128)S(1)} %copy-done.1, ...), custom_call_target="tpu_custom_call" | custom-call | tf_op jit(solution)/shard_map/lay_out/pallas_call | solution.py:544
  306.4 2.0 pick.1
  (138 shorter events, 54.1 us)
Async XLA Ops:
  11.4 6.2 %collective-permute-start.1 = (f32[192,128]{1,0:T(8,128)S(1)}, f32[192,128]{1,0:T(8,128)S(1)}, u32[]{:S(2)}, u32[]{:S(2)}) collective-permute-start(f32[192,128]{1,0:T(8,128)S(1)} %broadcast_select_fusion.8), channel_id=1, source_target_pairs={{0,4},{4,0},{8,12},{12,8},{1,5},{5,1},{9,13},{13,9},{2,6},{6,2},{1... | collective-permute-start | bytes 294920 | tf_op jit(solution)/shard_map/ppermute | solution.py:781
  14.4 5.8 %collective-permute-start.2 = (f32[192,128]{1,0:T(8,128)S(1)}, f32[192,128]{1,0:T(8,128)S(1)}, u32[]{:S(2)}, u32[]{:S(2)}) collective-permute-start(f32[192,128]{1,0:T(8,128)S(1)} %broadcast_select_fusion.8), channel_id=1, source_target_pairs={{0,8},{4,12},{8,0},{12,4},{1,9},{5,13},{9,1},{13,5},{2,10},{6,14},... | collective-permute-start | bytes 294920 | tf_op jit(solution)/shard_map/ppermute | solution.py:781
  16.0 5.5 %collective-permute-start.3 = (f32[192,128]{1,0:T(8,128)S(1)}, f32[192,128]{1,0:T(8,128)S(1)}, u32[]{:S(2)}, u32[]{:S(2)}) collective-permute-start(f32[192,128]{1,0:T(8,128)S(1)} %broadcast_select_fusion.8), channel_id=1, source_target_pairs={{0,12},{4,8},{8,4},{12,0},{1,13},{5,9},{9,5},{13,1},{2,14},{6,10},... | collective-permute-start | bytes 294920 | tf_op jit(solution)/shard_map/ppermute | solution.py:781
  38.9 1.7 collective-permute-start.5
  40.6 5.4 %collective-permute-start.6 = (f32[192,128]{1,0:T(8,128)S(1)}, f32[192,128]{1,0:T(8,128)S(1)}, u32[]{:S(2)}, u32[]{:S(2)}) collective-permute-start(f32[192,128]{1,0:T(8,128)S(1)} %broadcast_select_fusion.6), channel_id=1, source_target_pairs={{0,4},{4,0},{8,12},{12,8},{1,5},{5,1},{9,13},{13,9},{2,6},{6,2},{1... | collective-permute-start | bytes 294920 | tf_op jit(solution)/shard_map/ppermute | solution.py:781
  41.6 5.3 %collective-permute-start.7 = (f32[192,128]{1,0:T(8,128)S(1)}, f32[192,128]{1,0:T(8,128)S(1)}, u32[]{:S(2)}, u32[]{:S(2)}) collective-permute-start(f32[192,128]{1,0:T(8,128)S(1)} %broadcast_select_fusion.6), channel_id=1, source_target_pairs={{0,8},{4,12},{8,0},{12,4},{1,9},{5,13},{9,1},{13,5},{2,10},{6,14},... | collective-permute-start | bytes 294920 | tf_op jit(solution)/shard_map/ppermute | solution.py:781
  42.4 6.1 %collective-permute-start.8 = (f32[192,128]{1,0:T(8,128)S(1)}, f32[192,128]{1,0:T(8,128)S(1)}, u32[]{:S(2)}, u32[]{:S(2)}) collective-permute-start(f32[192,128]{1,0:T(8,128)S(1)} %broadcast_select_fusion.6), channel_id=1, source_target_pairs={{0,12},{4,8},{8,4},{12,0},{1,13},{5,9},{9,5},{13,1},{2,14},{6,10},... | collective-permute-start | bytes 294920 | tf_op jit(solution)/shard_map/ppermute | solution.py:781
  44.2 26.8 %collective-permute-start.15 = (f32[256,128]{1,0:T(8,128)S(1)}, f32[256,128]{1,0:T(8,128)S(1)}, u32[]{:S(2)}, u32[]{:S(2)}) collective-permute-start(f32[256,128]{1,0:T(8,128)S(1)} %copy-done.8), channel_id=1, source_target_pairs={{0,16},{16,0},{1,17},{17,1},{2,18},{18,2},{3,19},{19,3},{4,20},{20... | collective-permute-start | bytes 393224 | tf_op jit(solution)/shard_map/ppermute | solution.py:781
  48.7 26.8 %collective-permute-start.17 = (f32[256,256]{1,0:T(8,128)S(1)}, f32[256,256]{1,0:T(8,128)S(1)}, u32[]{:S(2)}, u32[]{:S(2)}) collective-permute-start(f32[256,256]{1,0:T(8,128)S(1)} %get-tuple-element.83.inv_any), channel_id=1, source_target_pairs={{0,16},{16,0},{1,17},{17,1},{2,18},{18,2},{3,19},{19,3},{4,20},{20... | collective-permute-start | bytes 786440 | tf_op jit(solution)/shard_map/ppermute | solution.py:781
  54.3 17.6 %collective-permute-start.10 = (f32[192,128]{1,0:T(8,128)S(1)}, f32[192,128]{1,0:T(8,128)S(1)}, u32[]{:S(2)}, u32[]{:S(2)}) collective-permute-start(f32[192,128]{1,0:T(8,128)S(1)} %get-tuple-element.86), channel_id=1, source_target_pairs={{0,16},{16,0},{1,17},{17,1},{2,18},{18,2},{3,19},{19,3},{4,20},{20... | collective-permute-start | bytes 294920 | tf_op jit(solution)/shard_map/ppermute | solution.py:781
  71.0 9.1 %collective-permute-start.16 = (f32[256,256]{1,0:T(8,128)S(1)}, f32[256,256]{1,0:T(8,128)S(1)}, u32[]{:S(2)}, u32[]{:S(2)}) collective-permute-start(f32[256,256]{1,0:T(8,128)S(1)} %get-tuple-element.82.low_any), channel_id=1, source_target_pairs={{0,16},{16,0},{1,17},{17,1},{2,18},{18,2},{3,19},{19,3},{4,20},{20... | collective-permute-start | bytes 786440 | tf_op jit(solution)/shard_map/ppermute | solution.py:781
  72.0 5.2 %collective-permute-start.11 = (f32[192,128]{1,0:T(8,128)S(1)}, f32[192,128]{1,0:T(8,128)S(1)}, u32[]{:S(2)}, u32[]{:S(2)}) collective-permute-start(f32[192,128]{1,0:T(8,128)S(1)} %broadcast_select_fusion.5), channel_id=1, source_target_pairs={{0,4},{4,0},{8,12},{12,8},{1,5},{5,1},{9,13},{13,9},{2,6},{6,2},{1... | collective-permute-start | bytes 294920 | tf_op jit(solution)/shard_map/ppermute | solution.py:781
  73.1 6.9 %collective-permute-start.12 = (f32[192,128]{1,0:T(8,128)S(1)}, f32[192,128]{1,0:T(8,128)S(1)}, u32[]{:S(2)}, u32[]{:S(2)}) collective-permute-start(f32[192,128]{1,0:T(8,128)S(1)} %broadcast_select_fusion.5), channel_id=1, source_target_pairs={{0,8},{4,12},{8,0},{12,4},{1,9},{5,13},{9,1},{13,5},{2,10},{6,14},... | collective-permute-start | bytes 294920 | tf_op jit(solution)/shard_map/ppermute | solution.py:781
  74.3 5.7 %collective-permute-start.13 = (f32[192,128]{1,0:T(8,128)S(1)}, f32[192,128]{1,0:T(8,128)S(1)}, u32[]{:S(2)}, u32[]{:S(2)}) collective-permute-start(f32[192,128]{1,0:T(8,128)S(1)} %broadcast_select_fusion.5), channel_id=1, source_target_pairs={{0,12},{4,8},{8,4},{12,0},{1,13},{5,9},{9,5},{13,1},{2,14},{6,10},... | collective-permute-start | bytes 294920 | tf_op jit(solution)/shard_map/ppermute | solution.py:781
  106.6 5.2 %collective-permute-start.19 = (f32[192,128]{1,0:T(8,128)S(1)}, f32[192,128]{1,0:T(8,128)S(1)}, u32[]{:S(2)}, u32[]{:S(2)}) collective-permute-start(f32[192,128]{1,0:T(8,128)S(1)} %broadcast_select_fusion.7), channel_id=1, source_target_pairs={{0,4},{4,0},{8,12},{12,8},{1,5},{5,1},{9,13},{13,9},{2,6},{6,2},{1... | collective-permute-start | bytes 294920 | tf_op jit(solution)/shard_map/ppermute | solution.py:781
  107.6 5.3 %collective-permute-start.20 = (f32[192,128]{1,0:T(8,128)S(1)}, f32[192,128]{1,0:T(8,128)S(1)}, u32[]{:S(2)}, u32[]{:S(2)}) collective-permute-start(f32[192,128]{1,0:T(8,128)S(1)} %broadcast_select_fusion.7), channel_id=1, source_target_pairs={{0,8},{4,12},{8,0},{12,4},{1,9},{5,13},{9,1},{13,5},{2,10},{6,14},... | collective-permute-start | bytes 294920 | tf_op jit(solution)/shard_map/ppermute | solution.py:781
  108.3 5.9 %collective-permute-start.21 = (f32[192,128]{1,0:T(8,128)S(1)}, f32[192,128]{1,0:T(8,128)S(1)}, u32[]{:S(2)}, u32[]{:S(2)}) collective-permute-start(f32[192,128]{1,0:T(8,128)S(1)} %broadcast_select_fusion.7), channel_id=1, source_target_pairs={{0,12},{4,8},{8,4},{12,0},{1,13},{5,9},{9,5},{13,1},{2,14},{6,10},... | collective-permute-start | bytes 294920 | tf_op jit(solution)/shard_map/ppermute | solution.py:781
  127.6 40.2 %collective-permute-start.24 = (f32[128,2048]{1,0:T(8,128)S(1)}, f32[128,2048]{1,0:T(8,128)S(1)}, u32[]{:S(2)}, u32[]{:S(2)}) collective-permute-start(f32[128,2048]{1,0:T(8,128)S(1)} %round_piece.6.refs_2_), channel_id=1, source_target_pairs={{0,2},{1,3},{2,0},{3,1},{4,6},{5,7},{6,4},{7,5},{8,10},{9,11},{10,... | collective-permute-start | bytes 3145736 | tf_op jit(solution)/shard_map/ppermute | solution.py:790
  134.9 49.6 %collective-permute-start.25 = (f32[128,2048]{1,0:T(8,128)S(1)}, f32[128,2048]{1,0:T(8,128)S(1)}, u32[]{:S(2)}, u32[]{:S(2)}) collective-permute-start(f32[128,2048]{1,0:T(8,128)S(1)} %round_piece.7.refs_3_), channel_id=1, source_target_pairs={{0,3},{1,2},{2,1},{3,0},{4,7},{5,6},{6,5},{7,4},{8,11},{9,10},{10,... | collective-permute-start | bytes 3145736 | tf_op jit(solution)/shard_map/ppermute | solution.py:790
  140.9 43.6 %collective-permute-start.23 = (f32[128,2048]{1,0:T(8,128)S(1)}, f32[128,2048]{1,0:T(8,128)S(1)}, u32[]{:S(2)}, u32[]{:S(2)}) collective-permute-start(f32[128,2048]{1,0:T(8,128)S(1)} %round_piece.5.refs_1_), channel_id=1, source_target_pairs={{0,1},{1,0},{2,3},{3,2},{4,5},{5,4},{6,7},{7,6},{8,9},{9,8},{10,11... | collective-permute-start | bytes 3145736 | tf_op jit(solution)/shard_map/ppermute | solution.py:790
  143.0 38.6 %collective-permute-start.26 = (f32[256,128]{1,0:T(8,128)S(1)}, f32[256,128]{1,0:T(8,128)S(1)}, u32[]{:S(2)}, u32[]{:S(2)}) collective-permute-start(f32[256,128]{1,0:T(8,128)S(1)} %get-tuple-element.93.front_ref.refs_4_), channel_id=1, source_target_pairs={{0,1},{1,0},{2,3},{3,2},{4,5},{5,4},{6,7},{7,6},{8,9},{9,8},{10,11... | collective-permute-start | bytes 393224 | tf_op jit(solution)/shard_map/ppermute | solution.py:790
  146.7 37.7 %collective-permute-start.27 = (f32[256,128]{1,0:T(8,128)S(1)}, f32[256,128]{1,0:T(8,128)S(1)}, u32[]{:S(2)}, u32[]{:S(2)}) collective-permute-start(f32[256,128]{1,0:T(8,128)S(1)} %get-tuple-element.93.front_ref.refs_4_), channel_id=1, source_target_pairs={{0,2},{1,3},{2,0},{3,1},{4,6},{5,7},{6,4},{7,5},{8,10},{9,11},{10,... | collective-permute-start | bytes 393224 | tf_op jit(solution)/shard_map/ppermute | solution.py:790
  167.7 16.7 %collective-permute-start.28 = (f32[256,128]{1,0:T(8,128)S(1)}, f32[256,128]{1,0:T(8,128)S(1)}, u32[]{:S(2)}, u32[]{:S(2)}) collective-permute-start(f32[256,128]{1,0:T(8,128)S(1)} %get-tuple-element.93.front_ref.refs_4_), channel_id=1, source_target_pairs={{0,3},{1,2},{2,1},{3,0},{4,7},{5,6},{6,5},{7,4},{8,11},{9,10},{10,... | collective-permute-start | bytes 393224 | tf_op jit(solution)/shard_map/ppermute | solution.py:790
  181.7 2.8 collective-permute-start.29
  194.3 1.7 collective-permute-start.30
  196.0 6.8 %collective-permute-start.31 = (f32[160,128]{1,0:T(8,128)S(1)}, f32[160,128]{1,0:T(8,128)S(1)}, u32[]{:S(2)}, u32[]{:S(2)}) collective-permute-start(f32[160,128]{1,0:T(8,128)S(1)} %get-tuple-element.111), channel_id=1, source_target_pairs={{0,4},{4,0},{8,12},{12,8},{1,5},{5,1},{9,13},{13,9},{2,6},{6,2},{1... | collective-permute-start | bytes 245768 | tf_op jit(solution)/shard_map/ppermute | solution.py:781
  197.2 7.3 %collective-permute-start.32 = (f32[160,128]{1,0:T(8,128)S(1)}, f32[160,128]{1,0:T(8,128)S(1)}, u32[]{:S(2)}, u32[]{:S(2)}) collective-permute-start(f32[160,128]{1,0:T(8,128)S(1)} %get-tuple-element.110), channel_id=1, source_target_pairs={{0,8},{4,12},{8,0},{12,4},{1,9},{5,13},{9,1},{13,5},{2,10},{6,14},... | collective-permute-start | bytes 245768 | tf_op jit(solution)/shard_map/ppermute | solution.py:781
  198.4 6.1 %collective-permute-start.33 = (f32[160,128]{1,0:T(8,128)S(1)}, f32[160,128]{1,0:T(8,128)S(1)}, u32[]{:S(2)}, u32[]{:S(2)}) collective-permute-start(f32[160,128]{1,0:T(8,128)S(1)} %get-tuple-element.109), channel_id=1, source_target_pairs={{0,12},{4,8},{8,4},{12,0},{1,13},{5,9},{9,5},{13,1},{2,14},{6,10},... | collective-permute-start | bytes 245768 | tf_op jit(solution)/shard_map/ppermute | solution.py:781
  199.6 67.3 %collective-permute-start.41 = (f32[128,2048]{1,0:T(8,128)}, f32[128,2048]{1,0:T(8,128)}, u32[]{:S(2)}, u32[]{:S(2)}) collective-permute-start(f32[128,2048]{1,0:T(8,128)} %get-tuple-element.97.refs_5_), channel_id=1, source_target_pairs={{16,17},{17,16},{18,19},{19,18},{20,21},{21,20},{22,23},{23,22},{2... | collective-permute-start | bytes 3145736 | tf_op jit(solution)/shard_map/ppermute | solution.py:790
  201.3 65.7 %collective-permute-start.42 = (f32[128,2048]{1,0:T(8,128)}, f32[128,2048]{1,0:T(8,128)}, u32[]{:S(2)}, u32[]{:S(2)}) collective-permute-start(f32[128,2048]{1,0:T(8,128)} %get-tuple-element.98.refs_6_), channel_id=1, source_target_pairs={{16,18},{17,19},{18,16},{19,17},{20,22},{21,23},{22,20},{23,21},{2... | collective-permute-start | bytes 3145736 | tf_op jit(solution)/shard_map/ppermute | solution.py:790
  202.9 64.0 %collective-permute-start.43 = (f32[128,2048]{1,0:T(8,128)}, f32[128,2048]{1,0:T(8,128)}, u32[]{:S(2)}, u32[]{:S(2)}) collective-permute-start(f32[128,2048]{1,0:T(8,128)} %get-tuple-element.99.refs_7_), channel_id=1, source_target_pairs={{16,19},{17,18},{18,17},{19,16},{20,23},{21,22},{22,21},{23,20},{2... | collective-permute-start | bytes 3145736 | tf_op jit(solution)/shard_map/ppermute | solution.py:790
  204.6 15.1 %collective-permute-start.34 = (f32[160,128]{1,0:T(8,128)S(1)}, f32[160,128]{1,0:T(8,128)S(1)}, u32[]{:S(2)}, u32[]{:S(2)}) collective-permute-start(f32[160,128]{1,0:T(8,128)S(1)} %fusion.1), channel_id=1, source_target_pairs={{0,1},{1,0},{2,3},{3,2},{4,5},{5,4},{6,7},{7,6},{8,9},{9,8},{10,11... | collective-permute-start | bytes 245768 | tf_op jit(solution)/shard_map/ppermute | solution.py:781
  205.3 14.8 %collective-permute-start.35 = (f32[160,128]{1,0:T(8,128)S(1)}, f32[160,128]{1,0:T(8,128)S(1)}, u32[]{:S(2)}, u32[]{:S(2)}) collective-permute-start(f32[160,128]{1,0:T(8,128)S(1)} %fusion.1), channel_id=1, source_target_pairs={{0,2},{1,3},{2,0},{3,1},{4,6},{5,7},{6,4},{7,5},{8,10},{9,11},{10,... | collective-permute-start | bytes 245768 | tf_op jit(solution)/shard_map/ppermute | solution.py:781
  219.7 7.2 %collective-permute-start.36 = (f32[160,128]{1,0:T(8,128)S(1)}, f32[160,128]{1,0:T(8,128)S(1)}, u32[]{:S(2)}, u32[]{:S(2)}) collective-permute-start(f32[160,128]{1,0:T(8,128)S(1)} %fusion.1), channel_id=1, source_target_pairs={{0,3},{1,2},{2,1},{3,0},{4,7},{5,6},{6,5},{7,4},{8,11},{9,10},{10,... | collective-permute-start | bytes 245768 | tf_op jit(solution)/shard_map/ppermute | solution.py:781
  226.9 4.5 %collective-permute-start.37 = (f32[160,128]{1,0:T(8,128)S(1)}, f32[160,128]{1,0:T(8,128)S(1)}, u32[]{:S(2)}, u32[]{:S(2)}) collective-permute-start(f32[160,128]{1,0:T(8,128)S(1)} %add_add_fusion.4), channel_id=1, source_target_pairs={{0,4},{4,0},{8,12},{12,8},{1,5},{5,1},{9,13},{13,9},{2,6},{6,2},{1... | collective-permute-start | bytes 245768 | tf_op jit(solution)/shard_map/ppermute | solution.py:781
  228.0 5.1 %collective-permute-start.38 = (f32[160,128]{1,0:T(8,128)S(1)}, f32[160,128]{1,0:T(8,128)S(1)}, u32[]{:S(2)}, u32[]{:S(2)}) collective-permute-start(f32[160,128]{1,0:T(8,128)S(1)} %add_add_fusion.4), channel_id=1, source_target_pairs={{0,8},{4,12},{8,0},{12,4},{1,9},{5,13},{9,1},{13,5},{2,10},{6,14},... | collective-permute-start | bytes 245768 | tf_op jit(solution)/shard_map/ppermute | solution.py:781
  231.4 5.3 %collective-permute-start.39 = (f32[160,128]{1,0:T(8,128)S(1)}, f32[160,128]{1,0:T(8,128)S(1)}, u32[]{:S(2)}, u32[]{:S(2)}) collective-permute-start(f32[160,128]{1,0:T(8,128)S(1)} %add_add_fusion.4), channel_id=1, source_target_pairs={{0,12},{4,8},{8,4},{12,0},{1,13},{5,9},{9,5},{13,1},{2,14},{6,10},... | collective-permute-start | bytes 245768 | tf_op jit(solution)/shard_map/ppermute | solution.py:781
  237.5 30.9 %collective-permute-start.40 = (f32[4,160,128]{2,1,0:T(8,128)}, f32[4,160,128]{2,1,0:T(8,128)}, u32[]{:S(2)}, u32[]{:S(2)}) collective-permute-start(f32[4,160,128]{2,1,0:T(8,128)} %pad_maximum_fusion.refs_8_.own_ref), channel_id=1, source_target_pairs={{0,16},{16,0},{1,17},{17,1},{2,18},{18,2},{3,19},{19,3},{4,20},{20... | collective-permute-start | bytes 983048 | tf_op jit(solution)/shard_map/ppermute | solution.py:781
  271.1 9.7 %collective-permute-start.44 = (f32[4,160,128]{2,1,0:T(8,128)S(1)}, f32[4,160,128]{2,1,0:T(8,128)S(1)}, u32[]{:S(2)}, u32[]{:S(2)}) collective-permute-start(f32[4,160,128]{2,1,0:T(8,128)S(1)} %get-tuple-element.104), channel_id=1, source_target_pairs={{0,16},{16,0},{1,17},{17,1},{2,18},{18,2},{3,19},{19,3},{4,20},{20... | collective-permute-start | bytes 983048 | tf_op jit(solution)/shard_map/ppermute | solution.py:781
  280.8 4.8 %collective-permute-start.45 = (f32[160,128]{1,0:T(8,128)S(1)}, f32[160,128]{1,0:T(8,128)S(1)}, u32[]{:S(2)}, u32[]{:S(2)}) collective-permute-start(f32[160,128]{1,0:T(8,128)S(1)} %get-tuple-element.107), channel_id=1, source_target_pairs={{0,4},{4,0},{8,12},{12,8},{1,5},{5,1},{9,13},{13,9},{2,6},{6,2},{1... | collective-permute-start | bytes 245768 | tf_op jit(solution)/shard_map/ppermute | solution.py:781
  282.0 4.4 %collective-permute-start.46 = (f32[160,128]{1,0:T(8,128)S(1)}, f32[160,128]{1,0:T(8,128)S(1)}, u32[]{:S(2)}, u32[]{:S(2)}) collective-permute-start(f32[160,128]{1,0:T(8,128)S(1)} %get-tuple-element.106), channel_id=1, source_target_pairs={{0,8},{4,12},{8,0},{12,4},{1,9},{5,13},{9,1},{13,5},{2,10},{6,14},... | collective-permute-start | bytes 245768 | tf_op jit(solution)/shard_map/ppermute | solution.py:781
  283.1 5.3 %collective-permute-start.47 = (f32[160,128]{1,0:T(8,128)S(1)}, f32[160,128]{1,0:T(8,128)S(1)}, u32[]{:S(2)}, u32[]{:S(2)}) collective-permute-start(f32[160,128]{1,0:T(8,128)S(1)} %get-tuple-element.105), channel_id=1, source_target_pairs={{0,12},{4,8},{8,4},{12,0},{1,13},{5,9},{9,5},{13,1},{2,14},{6,10},... | collective-permute-start | bytes 245768 | tf_op jit(solution)/shard_map/ppermute | solution.py:781
  289.2 4.5 %collective-permute-start.48 = (f32[64,128]{1,0:T(8,128)S(1)}, f32[64,128]{1,0:T(8,128)S(1)}, u32[]{:S(2)}, u32[]{:S(2)}) collective-permute-start(f32[64,128]{1,0:T(8,128)S(1)} %get-tuple-element.114), channel_id=1, source_target_pairs={{0,1},{1,0},{2,3},{3,2},{4,5},{5,4},{6,7},{7,6},{8,9},{9,8},{10,11... | collective-permute-start | bytes 98312 | tf_op jit(solution)/shard_map/ppermute | solution.py:781
  290.7 5.4 %collective-permute-start.49 = (f32[64,128]{1,0:T(8,128)S(1)}, f32[64,128]{1,0:T(8,128)S(1)}, u32[]{:S(2)}, u32[]{:S(2)}) collective-permute-start(f32[64,128]{1,0:T(8,128)S(1)} %get-tuple-element.113), channel_id=1, source_target_pairs={{0,2},{1,3},{2,0},{3,1},{4,6},{5,7},{6,4},{7,5},{8,10},{9,11},{10,... | collective-permute-start | bytes 98312 | tf_op jit(solution)/shard_map/ppermute | solution.py:781
  292.5 5.7 %collective-permute-start.50 = (f32[64,128]{1,0:T(8,128)S(1)}, f32[64,128]{1,0:T(8,128)S(1)}, u32[]{:S(2)}, u32[]{:S(2)}) collective-permute-start(f32[64,128]{1,0:T(8,128)S(1)} %get-tuple-element.112), channel_id=1, source_target_pairs={{0,3},{1,2},{2,1},{3,0},{4,7},{5,6},{6,5},{7,4},{8,11},{9,10},{10,... | collective-permute-start | bytes 98312 | tf_op jit(solution)/shard_map/ppermute | solution.py:781
  298.2 6.7 %collective-permute-start.51 = (f32[64,128]{1,0:T(8,128)S(1)}, f32[64,128]{1,0:T(8,128)S(1)}, u32[]{:S(2)}, u32[]{:S(2)}) collective-permute-start(f32[64,128]{1,0:T(8,128)S(1)} %fusion.3), channel_id=1, source_target_pairs={{0,4},{4,0},{8,12},{12,8},{1,5},{5,1},{9,13},{13,9},{2,6},{6,2},{1... | collective-permute-start | bytes 98312 | tf_op jit(solution)/shard_map/ppermute | solution.py:781
  298.9 6.0 %collective-permute-start.52 = (f32[64,128]{1,0:T(8,128)S(1)}, f32[64,128]{1,0:T(8,128)S(1)}, u32[]{:S(2)}, u32[]{:S(2)}) collective-permute-start(f32[64,128]{1,0:T(8,128)S(1)} %fusion.3), channel_id=1, source_target_pairs={{0,8},{4,12},{8,0},{12,4},{1,9},{5,13},{9,1},{13,5},{2,10},{6,14},... | collective-permute-start | bytes 98312 | tf_op jit(solution)/shard_map/ppermute | solution.py:781
  300.1 4.9 %collective-permute-start.53 = (f32[64,128]{1,0:T(8,128)S(1)}, f32[64,128]{1,0:T(8,128)S(1)}, u32[]{:S(2)}, u32[]{:S(2)}) collective-permute-start(f32[64,128]{1,0:T(8,128)S(1)} %fusion.3), channel_id=1, source_target_pairs={{0,12},{4,8},{8,4},{12,0},{1,13},{5,9},{9,5},{13,1},{2,14},{6,10},... | collective-permute-start | bytes 98312 | tf_op jit(solution)/shard_map/ppermute | solution.py:781
  (19 other events, 214.9 us)
